TPU v7x, 256 devices: a whole 4x4x8 slice. The times are simulated.
256 devices in a mesh: alpha: 4 (over x), beta: 64 (over z, y, core).
Axes of the slice: x: 4, y: 4, z: 8, core: 2. Of those that a mesh axis runs over, the one named last changes fastest.
Arguments:
- civec: float32 [1024, 24576], P('alpha', 'beta'), may hold values from -6 to 6
- batch_index: int32 [8], replicated, may hold values from 0 to 1023, as said below
- exc_alpha: int32 [3, 8, 81], replicated, may hold values from -1 to 1023, as said below
- exc_beta: int32 [3, 24576, 81], P(None, 'beta'), may hold values from -1 to 24575, as said below
- one_body: float32 [324], replicated, may hold values from -0.625 to 0.625
Outputs:
- sigma: float32 [8, 24576], P('alpha', 'beta')
- density_one: float32 [2, 324], replicated
- rdm_same: float32 [324, 324], replicated
- rdm_mixed: float32 [324, 324], replicated
Inputs may be any that keep to these rules, and one draw needn't show every extreme that they name: `batch_index`: entries b * 2 to (b + 1) * 2 - 1 for b = 0..3 are distinct strings of the block b * 256 to (b + 1) * 256 - 1. `exc_alpha`: plane 0 holds source alpha strings below 1024, plane 1 pair indices below 324, distinct within each row, plane 2 signs -1, 0 or 1; a slot with sign 0 is empty, live slots come first, every row has at least 40 live slots and some row has all 81. `exc_beta`: plane 0 holds source beta strings below 24576, plane 1 pair indices below 324, distinct within each row, plane 2 signs -1, 0 or 1; a slot with sign 0 is empty, live slots come first, every row has at least 40 live slots and some row has all 81.
All inputs are finite; a program needn't handle non-finite values.
Results may differ from a plain program's by a relative error of at most 0.0003.
Values sent between devices are 32-bit elements; how exact they have to be, the bound alone decides.
A program may use at most 192 MiB of HBM per device.

v0:
```python
import math

import jax
import jax.numpy as jnp
from jax import lax
from jax.sharding import PartitionSpec as P

BLOCK = 2


def body(civec, batch_index, exc_alpha, exc_beta, one_body):
    highest = lax.Precision.HIGHEST
    group_id = lax.axis_index("alpha")
    groups = lax.axis_size("alpha")
    rows_dev = civec.shape[0]
    beta_dev = civec.shape[1]
    total_batch = batch_index.shape[0]
    batch_size = total_batch // groups
    slot_count = exc_alpha.shape[2]
    pair_count = one_body.shape[0]
    my_batch = lax.dynamic_slice_in_dim(batch_index, group_id * batch_size, batch_size)
    batch_rows = civec[my_batch - group_id * rows_dev]
    my_exc = lax.dynamic_slice_in_dim(exc_alpha, group_id * batch_size, batch_size, 1)
    sources = my_exc[0]
    gathered = lax.all_gather(civec, "alpha", axis=0, tiled=True)
    alpha_rows = gathered[sources]
    beta_sources = exc_beta[0]
    spread = lax.all_gather(batch_rows, "beta", axis=1, tiled=True)
    beta_picked = spread[:, beta_sources]
    beta_values = beta_picked * exc_beta[2].astype(jnp.float32)[None]
    pair_range = jnp.arange(pair_count, dtype=jnp.int32)
    placing = (my_exc[1][..., None] == pair_range[None, None, :]).astype(jnp.float32) * my_exc[
        2
    ].astype(jnp.float32)[..., None]
    blocks = batch_size // BLOCK
    columns = jnp.arange(beta_dev, dtype=jnp.int32)[:, None]
    beta_pairs = exc_beta[1]

    def block_step(totals, inputs):
        place_blk, rows_blk, values_blk, batch_blk = inputs
        d_alpha = jnp.einsum("bep,ben->bpn", place_blk, rows_blk, precision=highest)
        d_beta = (
            jnp.zeros((BLOCK, pair_count, beta_dev), jnp.float32)
            .at[:, beta_pairs, columns]
            .add(values_blk)
        )
        sigma_blk = jnp.einsum("p,bpn->bn", one_body, d_alpha + d_beta, precision=highest)
        one_part = jnp.stack(
            [
                jnp.einsum("bpn,bn->p", d_alpha, batch_blk, precision=highest),
                jnp.einsum("bpn,bn->p", d_beta, batch_blk, precision=highest),
            ]
        )
        same_part = jnp.einsum("bpn,bqn->pq", d_alpha, d_alpha, precision=highest)
        mixed_part = jnp.einsum("bpn,bqn->pq", d_alpha, d_beta, precision=highest)
        return ((totals[0] + one_part, totals[1] + same_part, totals[2] + mixed_part), sigma_blk)

    start_totals = (
        jnp.zeros((2, pair_count), jnp.float32),
        jnp.zeros((pair_count, pair_count), jnp.float32),
        jnp.zeros((pair_count, pair_count), jnp.float32),
    )
    block_inputs = (
        placing.reshape(blocks, BLOCK, slot_count, pair_count),
        alpha_rows.reshape(blocks, BLOCK, slot_count, beta_dev),
        beta_values.reshape(blocks, BLOCK, beta_dev, slot_count),
        batch_rows.reshape(blocks, BLOCK, beta_dev),
    )
    totals, sigma_rows = lax.scan(block_step, start_totals, block_inputs)
    sigma_rows = sigma_rows.reshape(batch_size, beta_dev)
    one_total, same_total, mixed_total = lax.psum(
        (totals[0], totals[1], totals[2]), ("alpha", "beta")
    )
    norm_count = total_batch * beta_dev * lax.axis_size("beta")
    root_count = math.sqrt(norm_count)
    return (sigma_rows, one_total / root_count, same_total / norm_count, mixed_total / root_count)


def solution(mesh):
    in_specs = (P("alpha", "beta"), P(), P(), P(None, "beta", None), P())
    out_specs = (P("alpha", "beta"), P(), P(), P())
    return jax.shard_map(body, mesh=mesh, in_specs=in_specs, out_specs=out_specs, check_vma=False)
```

profile of v0, /device:TPU:1, one launch (start us, length us, event | category | flops | bytes accessed | tf_op | source)
XLA Modules:
  0.0 846.4 jit_solution(15939392918456565759)
XLA Ops:
  8.0 0.7 compare_select_fusion.2
  8.7 0.7 compare_select_fusion.3
  9.5 1.6 gather_fusion.1
  11.0 48.8 %all-gather = f32[2,24576]{1,0:T(2,128)S(1)} all-gather(f32[2,384]{1,0:T(2,128)S(1)} %gather_fusion.1), channel_id=2, replica_groups=mesh['alpha'=4,'beta'=64] {'beta'}, dimensions={1}, use_global_device_ids=true | all-gather | bytes 199680 | tf_op jit(solution)/shard_map/all_gather | solution.py:28
  59.9 6.8 copy.20
  66.6 1.0 compare_select_fusion
  68.0 62.3 %gather_fusion.2 = f32[31104,2]{1,0:T(8,128)} fusion(f32[2,24576]{0,1:T(8,128)} %copy.20, s32[31744]{0:T(1024)S(1)} %pad_clamp_fusion.1), kind=kCustom, calls=%fused_computation.2 | custom fusion | bytes 622080 | tf_op jit(solution)/shard_map/gather | solution.py:29
  130.4 9.0 %copy.21 = f32[31104,2]{0,1:T(2,128)S(1)} copy(f32[31104,2]{1,0:T(8,128)} %gather_fusion.2) | data formatting | bytes 497664 | tf_op jit(solution)/shard_map/gather | solution.py:29
  140.0 0.9 convert_bitcast_fusion
  141.6 8.1 copy.23
  150.4 10.4 %sort = (s32[31104]{0:T(1024)S(1)}, s32[31104]{0:T(1024)S(1)}) sort(s32[31104]{0:T(1024)S(1)} %reshape.143, s32[31104]{0:T(1024)S(1)} %iota.7), dimensions={0}, to_apply=%compare | sort | flops 466560 | bytes 497664
  160.9 374.1 %scatter_custom_fusion = f32[124416,2]{1,0:T(8,128)} fusion(s32[31104]{0:T(1024)S(1)} %get-tuple-element.28, f32[]{:T(128)} %constant.22.clone.1, f32[31104,2]{1,0:T(8,128)} %copy.23, s32[31744]{0:T(1024)S(1)} %pad_clamp_fusion), kind=kCustom, calls=%fused_computation.5 | custom fusion | flops 62208 | bytes 995840
  535.0 35.2 %copy.27 = f32[324,384,2]{1,0,2:T(8,128)S(1)} copy(f32[324,384,2]{2,1,0:T(8,128)} %bitcast.48) | data formatting | bytes 1990656
  570.2 0.7 dynamic-slice_bitcast_fusion.1
  570.9 0.9 convolution_bitcast_fusion.2
  571.8 2.4 gather_fusion
  574.2 1.4 fusion.9
  575.7 2.6 convolution_bitcast_fusion
  578.2 2.6 convolution_bitcast_fusion.1
  580.8 0.7 fusion.8
  582.1 0.9 convolution_bitcast_fusion.3
  583.0 75.3 %psum.21 = f32[2,324]{1,0:T(2,128)S(1)} all-reduce(f32[2,324]{1,0:T(2,128)S(1)} %pad_maximum_fusion), channel_id=1, replica_groups=mesh['alpha'=4,'beta'=64] {'alpha','beta'}, use_global_device_ids=true, to_apply=%region_1.2 | all-reduce | flops 648 | bytes 5184 | tf_op jit(solution)/shard_map/psum | solution.py:71
  658.9 178.0 %all-reduce.3.cloned.1.call-done = (f32[324,324]{1,0:T(8,128)}, f32[324,324]{1,0:T(8,128)}) async-done(((f32[324,324]{1,0:T(8,128)}, f32[324,324]{1,0:T(8,128)}), (f32[324,324]{1,0:T(8,128)}, f32[324,324]{1,0:T(8,128)})) %all-reduce.3.cloned.1.call-update) | async-done | bytes 839824 | tf_op jit(solution)/shard_map/psum | solution.py:71
  836.9 2.2 broadcast_multiply_fusion
  (34 shorter events, 4.4 us)
Async XLA Ops:
  7.2 564.7 %all-gather.3.cloned.1.call-start = ((), (), s32[]{:S(2)}) async-start(), calls=%async_computation | async-start | bytes 1966080 | tf_op jit(solution)/shard_map/all_gather | solution.py:25
  7.9 829.0 %all-reduce.3.cloned.1.call-start = ((), (), s32[]{:S(2)}) async-start(), calls=%async_computation.1 | async-start | bytes 2015232 | tf_op jit(solution)/shard_map/psum | solution.py:71
  130.4 19.4 %copy-start.2 = (s32[2]{0:T(128)S(1)}, s32[2]{0:T(128)}, u32[]{:S(2)}) copy-start(s32[2]{0:T(128)} %constant.40) | copy-start | bytes 28
  130.4 19.5 %copy-start.1 = (s32[2]{0:T(128)S(1)}, s32[2]{0:T(128)}, u32[]{:S(2)}) copy-start(s32[2]{0:T(128)} %constant.62) | copy-start | bytes 28
  534.9 35.3 %copy-start = (f32[324]{0:T(512)S(1)}, f32[324]{0:T(512)}, u32[]{:S(2)}) copy-start(f32[324]{0:T(512)} %param.9) | copy-start | bytes 3892
Sparse Core Ops, SparseCore 0:
  9.8 32.5 all-gather.2
  582.2 254.6 all-reduce.2
where the time goes:
time: 858 us; the launch traced here: 846 us
  other arithmetic  392 us (46%)
  waiting for transfers between devices  179 us (21%)
  local copies, waits for them, and re-layouts  128 us (15%)
  blocking collectives  124 us (14%)
  between operations  14.7 us (2%)
  matrix products  9.02 us (1%)
    unnamed x6, other arithmetic  385 us
    psum x1, waiting for transfers between devices, body(): lax.psum((totals[0], totals[1], totals[2]), ('alpha', 'beta'))  178 us
    psum x1, blocking collectives, body(): lax.psum((totals[0], totals[1], totals[2]), ('alpha', 'beta'))  75.3 us
    gather x3, local copies, waits for them, and re-layouts, body(): beta_picked = spread[:, beta_sources]  71.9 us
    all_gather x1, blocking collectives, body(): spread = lax.all_gather(batch_rows, 'beta', axis=1, tiled=True)  48.8 us
    unnamed x11, local copies, waits for them, and re-layouts  35.6 us
  transfers between devices with their start and end apart: 2, of which 1 were waited for; matrix products, arithmetic and copies ran while one was open for 61% of the time, Pallas kernels for 0%

commit v1 on v0

v1 whole, which is shorter than its diff:
```python
import functools
import math

import jax
import jax.numpy as jnp
from jax import lax
from jax.experimental import pallas as pl
from jax.experimental.pallas import tpu as pltpu
from jax.sharding import PartitionSpec as P

MESH = pl.DeviceIdType.MESH
F32, BF16, I32 = jnp.float32, jnp.bfloat16, jnp.int32
LANES = 128
HALF = 42
SHIFT = 68
ROWS = 168
NT = (((1,), (1,)), ((), ()))
NN = (((1,), (0,)), ((), ()))


def split(x):
    high = x.astype(BF16)
    return high, (x - high.astype(F32)).astype(BF16)


def dot(a, b, dims):
    return lax.dot_general(a, b, dims, preferred_element_type=F32)


def dot3(a, b, dims):
    return dot(a[0], b[0], dims) + (dot(a[0], b[1], dims) + dot(a[1], b[0], dims))


def dot2(a, b, dims):
    return dot(a, b[0], dims) + dot(a, b[1], dims)


def barrel(x, amount, bits, width):
    for bit in range(bits):
        moved = pltpu.roll(x, 1 << bit, 1)
        x = jnp.where(lax.rem(lax.div(amount, 1 << bit), 2) == 1, moved, x)
    return x


def spread_kernel(groups, parts, rows_ref, civ_ref, table_ref, blocks_ref, own_sem, ssem, rsem, xs, xr):
    ga = lax.axis_index("alpha")
    me = lax.axis_index("beta")
    barrier = pltpu.get_barrier_semaphore()

    def greet(d, c):
        pl.semaphore_signal(barrier, inc=1, device_id=(ga, lax.rem(me + d, parts)), device_id_type=MESH)
        return c

    lax.fori_loop(1, parts, greet, 0)
    for d in range(1, groups):
        pl.semaphore_signal(barrier, inc=1, device_id=(lax.rem(ga + d, groups), me), device_id_type=MESH)
    pl.semaphore_wait(barrier, parts - 1 + groups - 1)

    def row_copy(j, slot):
        return pltpu.make_async_remote_copy(
            rows_ref, table_ref.at[slot], ssem.at[j], rsem.at[slot], device_id=(ga, j), device_id_type=MESH
        )

    def send(d, c):
        row_copy(lax.rem(me + d, parts), me).start()
        return c

    lax.fori_loop(1, parts, send, 0)
    own = pltpu.make_async_copy(rows_ref, table_ref.at[me], own_sem)
    own.start()
    blocks = []
    for d in range(1, groups):
        copy = pltpu.make_async_remote_copy(
            civ_ref, blocks_ref.at[groups - 1 - d], xs.at[d - 1], xr.at[groups - 1 - d],
            device_id=(lax.rem(ga + d, groups), me), device_id_type=MESH,
        )
        copy.start()
        blocks.append(copy)
    own.wait()

    def finish(d, c):
        j = lax.rem(me + d, parts)
        copy = row_copy(j, j)
        copy.wait_send()
        copy.wait_recv()
        return c

    lax.fori_loop(1, parts, finish, 0)
    for copy in blocks:
        copy.wait_send()
    for d in range(1, groups):
        blocks[d - 1].wait_recv()


def pick_kernel(parts, slots, batch, src_ref, sign_ref, local_ref, code_ref, table_ref, civ_ref, blocks_ref, rows_ref,
                vals_ref, a_ref):
    ga = lax.axis_index("alpha")
    groups = lax.axis_size("alpha")
    rows_dev = civ_ref.shape[0]
    deep = code_ref.shape[1]
    tiles = deep // 8
    for lt in range(3):
        codes = [code_ref[lt, pl.ds(8 * i, 8), :] for i in range(tiles)]
        low = [jnp.bitwise_and(c, 127) for c in codes]
        high = [jnp.bitwise_and(lax.shift_right_logical(c, 7), 255) for c in codes]

        def step(j, acc):
            acc = list(acc)
            for t in range(3):
                row0 = jnp.broadcast_to(table_ref[j, pl.ds(t, 1), :], (8, LANES))
                row1 = jnp.broadcast_to(table_ref[j, pl.ds(3 + t, 1), :], (8, LANES))
                for i in range(tiles):
                    hit = high[i] == 3 * j + t
                    acc[2 * i] = jnp.where(hit, jnp.take_along_axis(row0, low[i], 1, mode="promise_in_bounds"), acc[2 * i])
                    acc[2 * i + 1] = jnp.where(hit, jnp.take_along_axis(row1, low[i], 1, mode="promise_in_bounds"), acc[2 * i + 1])
            return tuple(acc)

        acc = lax.fori_loop(0, parts, step, (jnp.zeros((8, LANES), F32),) * (2 * tiles))
        for i in range(tiles):
            sign = (lax.shift_right_logical(codes[i], 24) - 1).astype(F32)
            vals_ref[0, lt, pl.ds(8 * i, 8), :] = acc[2 * i] * sign
            vals_ref[1, lt, pl.ds(8 * i, 8), :] = acc[2 * i + 1] * sign

    a_ref[...] = jnp.zeros_like(a_ref)

    def take(k, c):
        for b in range(batch):
            source = src_ref[b * slots + k]
            away = lax.rem(lax.div(source, rows_dev) - ga + groups, groups)
            inner = lax.rem(source, rows_dev)
            mine = civ_ref[pl.ds(inner, 1), :]
            other = blocks_ref[jnp.maximum(away - 1, 0), pl.ds(inner, 1), :]
            sign = sign_ref[b * slots + k].astype(F32)
            a_ref[pl.ds(b * (slots + 1) + k, 1), :] = jnp.where(away == 0, mine, other) * sign
        return c

    lax.fori_loop(0, slots, take, 0)
    for b in range(batch):
        inner = local_ref[b]
        a_ref[pl.ds(b * (slots + 1) + slots, 1), :] = civ_ref[pl.ds(inner, 1), :]


def reduce_kernel(groups, shape, slots, pairs, vals_ref, code_ref, a_ref, own_pair_ref, pair_ref, ext_ref, hrow_ref, hcol_ref,
                  sigma_ref, mixed_ref, same_ref,
                  d_ref, tiles_ref, got_ref, zbuf, gat, all_ref,
                  ssem, rsem, zs, zr, fs, fr, cs, cr):
    nz, ny, nc = shape
    parts = nz * ny * nc
    per = 64 // parts
    ga = lax.axis_index("alpha")
    me = lax.axis_index("beta")
    z, y, core = me // (ny * nc), (me // nc) % ny, me % nc
    planes = groups * ny

    def at(zz, yy, cc):
        return (zz * ny + yy) * nc + cc

    barrier = pltpu.get_barrier_semaphore()

    def greet(d, c):
        pl.semaphore_signal(barrier, inc=1, device_id=(ga, lax.rem(me + d, parts)), device_id_type=MESH)
        return c

    lax.fori_loop(1, parts, greet, 0)
    around = []
    for k in range(1, planes):
        around.append((lax.rem(ga + k // ny, groups), lax.rem(y + k % ny, ny)))
    extra = 0
    for k, (aa, yy) in enumerate(around, 1):
        if k // ny:
            pl.semaphore_signal(barrier, inc=1, device_id=(aa, at(z, yy, core)), device_id_type=MESH)
            extra += 1

    width = a_ref.shape[1]
    deep = d_ref.shape[1]
    step_rows = 112
    for lt in range(width // LANES):
        cut = pl.ds(lt * LANES, LANES)
        for base in range(0, deep, step_rows):
            size = min(step_rows, deep - base)
            ids = lax.broadcasted_iota(I32, (size, LANES), 0) + base

            def place(e, acc):
                hit = jnp.bitwise_and(lax.shift_right_logical(code_ref[lt, pl.ds(e, 1), :], 15), 511) == ids
                return (
                    jnp.where(hit, vals_ref[0, lt, pl.ds(e, 1), :], acc[0]),
                    jnp.where(hit, vals_ref[1, lt, pl.ds(e, 1), :], acc[1]),
                )

            acc = lax.fori_loop(0, slots, place, (jnp.zeros((size, LANES), F32),) * 2)
            d_ref[0, pl.ds(base, size), cut] = acc[0]
            d_ref[1, pl.ds(base, size), cut] = acc[1]

    a = a_ref[...]
    a2 = split(a)
    d2 = [split(d_ref[b]) for b in range(2)]
    string = slots + 1
    row = lax.broadcasted_iota(I32, (ROWS, 1), 0)
    first = row < string
    col_row = lax.broadcasted_iota(I32, (1, ROWS), 1)
    one_hot = (lax.broadcasted_iota(I32, (deep, ROWS), 0) == own_pair_ref[...]).astype(F32)
    weight = jnp.sum(one_hot * hcol_ref[...], axis=0, keepdims=True)
    own_first = jnp.broadcast_to(jnp.where(col_row < string, weight, 0.0), (8, ROWS))
    own_second = jnp.broadcast_to(jnp.where(col_row < string, 0.0, weight), (8, ROWS))
    hrow = split(jnp.broadcast_to(hrow_ref[...], (8, deep)))
    sigma_ref[0:1, :] = (dot3(split(own_first), a2, NN) + dot3(hrow, d2[0], NN))[0:1]
    sigma_ref[1:2, :] = (dot3(split(own_second), a2, NN) + dot3(hrow, d2[1], NN))[0:1]
    m = jnp.where(first, dot3(a2, d2[0], NT), dot3(a2, d2[1], NT))
    ext_i = lax.broadcasted_iota(I32, (LANES, ROWS), 0)
    ext_j = lax.broadcasted_iota(I32, (LANES, ROWS), 1)
    wrapped = jnp.where(ext_i >= string, ext_i - string, ext_i)
    grams = []
    for b in range(2):
        perm = (ext_j == wrapped + b * string).astype(BF16)
        ext = tuple(dot(perm, part, NN).astype(BF16) for part in a2)
        grams.append(dot3(a2, ext, NT))
    gram = jnp.where(first, grams[0], grams[1])
    local = jnp.where(first, row, row - string)
    folded = barrel(gram, lax.rem(SHIFT - local + 2 * LANES, LANES), 7, LANES)
    lane = lax.broadcasted_iota(I32, (ROWS, LANES), 1)
    tail = jnp.concatenate([m[:, 2 * LANES :], jnp.zeros((ROWS, 3 * LANES - deep), F32)], axis=1)
    last = jnp.where(lane < SHIFT, tail, jnp.where(lane < SHIFT + HALF, folded, 0.0))
    for rg in range(ROWS // 8):
        for lt in range(3):
            k = rg * 3 + lt
            piece = last if lt == 2 else m[:, lt * LANES : (lt + 1) * LANES]
            tiles_ref[k // per, k % per] = piece[8 * rg : 8 * rg + 8]
    tiles_ref[parts - 1, per - 1] = jnp.zeros((8, LANES), F32)

    pl.semaphore_wait(barrier, parts - 1 + extra)

    def part_copy(j, slot):
        return pltpu.make_async_remote_copy(
            tiles_ref.at[j], got_ref.at[slot], ssem.at[j], rsem.at[slot], device_id=(ga, j), device_id_type=MESH
        )

    def send(d, c):
        part_copy(lax.rem(me + d, parts), me).start()
        return c

    lax.fori_loop(1, parts, send, 0)
    got_ref[me] = tiles_ref[me]

    def finish(d, c):
        j = lax.rem(me + d, parts)
        part_copy(j, j).wait_recv()
        return c

    lax.fori_loop(1, parts, finish, 0)
    zbuf[z] = jnp.sum(got_ref[...], axis=0)

    def z_copy(zz, slot):
        return pltpu.make_async_remote_copy(
            zbuf.at[slot], zbuf.at[slot], zs.at[zz], zr.at[slot], device_id=(ga, at(zz, y, core)), device_id_type=MESH
        )

    for k in range(1, nz):
        z_copy(lax.rem(z + k, nz), z).start()
    for k in range(1, nz):
        zz = lax.rem(z + k, nz)
        z_copy(zz, zz).wait_recv()

    def plane_copy(src, aa, yy, slot_a, slot_y):
        return pltpu.make_async_remote_copy(
            src, gat.at[slot_a, slot_y, core], fs.at[aa, yy], fr.at[slot_a, slot_y],
            device_id=(aa, at(z, yy, core)), device_id_type=MESH,
        )

    def twin_copy(src, slot_a, slot_y, slot_c):
        return pltpu.make_async_remote_copy(
            src, gat.at[slot_a, slot_y, slot_c], cs.at[slot_a, slot_y], cr.at[slot_a, slot_y],
            device_id=(ga, at(z, y, 1 - core)), device_id_type=MESH,
        )

    for aa, yy in around:
        plane_copy(zbuf, aa, yy, ga, y).start()
    twin_copy(zbuf, ga, y, core).start()
    gat[ga, y, core] = zbuf[...]
    for aa, yy in around:
        plane_copy(zbuf, aa, yy, aa, yy).wait_recv()
        twin_copy(gat.at[aa, yy, core], aa, yy, core).start()
    for aa, yy in [(ga, y)] + around:
        twin_copy(zbuf, aa, yy, 1 - core).wait_recv()

    for a_ in range(groups):
        for rg in range(ROWS // 8):
            for lt in range(3):
                k = rg * 3 + lt
                j, s = k // per, k % per
                all_ref[pl.ds(a_ * ROWS + 8 * rg, 8), pl.ds(lt * LANES, LANES)] = gat[
                    a_, (j // nc) % ny, j % nc, j // (ny * nc), s
                ]
    placing = (lax.broadcasted_iota(I32, (deep, groups * ROWS), 0) == pair_ref[...]).astype(BF16)
    mixed_ref[...] = dot2(placing, split(all_ref[...]), NN)
    weights = jnp.where((lane == SHIFT) | (lane == SHIFT + HALF - 1), 0.5, 1.0)
    weights = jnp.where((lane >= SHIFT) & (lane < SHIFT + HALF), weights, 0.0)
    amount = lax.rem(local - SHIFT + 2 * LANES, LANES)
    for a_ in range(groups):
        half = all_ref[pl.ds(a_ * ROWS, ROWS), pl.ds(2 * LANES, LANES)] * weights
        half = barrel(half, amount, 7, LANES)
        both = jnp.concatenate([jnp.where(first, half, 0.0), jnp.where(first, 0.0, half)], axis=1)
        right = (lax.broadcasted_iota(I32, (3 * LANES, 2 * LANES), 0) == ext_ref[pl.ds(a_, 1), :]).astype(BF16)
        all_ref[pl.ds(a_ * ROWS, ROWS), :] = sum(dot(p, right, NT) for p in split(both))
    upper = dot2(placing, split(all_ref[...]), NN)
    square = jnp.concatenate([upper, jnp.zeros((3 * LANES - deep, 3 * LANES), F32)], axis=0)
    same_ref[...] = (square + square.T)[:deep]

    def drain(d, c):
        j = lax.rem(me + d, parts)
        part_copy(j, j).wait_send()
        return c

    lax.fori_loop(1, parts, drain, 0)
    for k in range(1, nz):
        z_copy(lax.rem(z + k, nz), z).wait_send()
    for aa, yy in around:
        plane_copy(zbuf, aa, yy, ga, y).wait_send()
    for aa, yy in [(ga, y)] + around:
        twin_copy(zbuf, aa, yy, core).wait_send()


def body(shape, civec, batch_index, exc_alpha, exc_beta, one_body):
    vmem = pl.BlockSpec(memory_space=pltpu.VMEM)
    smem = pl.BlockSpec(memory_space=pltpu.SMEM)
    anywhere = pl.BlockSpec(memory_space=pl.ANY)
    nz, ny, nc = shape
    parts = nz * ny * nc
    per = 64 // parts
    ga = lax.axis_index("alpha")
    groups = lax.axis_size("alpha")
    rows_dev, width = civec.shape
    total = batch_index.shape[0]
    batch = total // groups
    slots = exc_alpha.shape[2]
    pairs = one_body.shape[0]
    deep = -(-pairs // 8) * 8
    slots_deep = -(-slots // 8) * 8
    local = lax.dynamic_slice_in_dim(batch_index, ga * batch, batch) - ga * rows_dev
    mine = lax.dynamic_slice_in_dim(exc_alpha, ga * batch, batch, 1)
    batch_rows = jnp.concatenate([lax.dynamic_slice_in_dim(civec, local[b], 1, 0) for b in range(batch)], 0)
    code = exc_beta[0] + exc_beta[1] * 32768 + (exc_beta[2] + 1) * (1 << 24)
    code = jnp.pad(code.T, ((0, slots_deep - slots), (0, 0)), constant_values=(511 << 15) + (1 << 24))
    code = code.reshape(slots_deep, 3, LANES).swapaxes(0, 1)
    pair_all = jnp.pad(exc_alpha[1], ((0, 0), (0, 1)), constant_values=pairs)
    pair_rows = jnp.pad(pair_all.reshape(groups, batch * (slots + 1)), ((0, 0), (0, ROWS - batch * (slots + 1))), constant_values=511)
    own_pair = lax.dynamic_slice_in_dim(pair_rows, ga, 1, 0)
    ext = jnp.concatenate([pair_all, pair_all[:, : LANES - slots - 1]], axis=1).reshape(groups, batch * LANES)
    hpad = jnp.pad(one_body, (0, deep - pairs))

    table, blocks = pl.pallas_call(
        functools.partial(spread_kernel, groups, parts),
        out_shape=(
            jax.ShapeDtypeStruct((parts, 6, LANES), F32),
            jax.ShapeDtypeStruct((groups - 1, rows_dev, width), F32),
        ),
        in_specs=[vmem, anywhere],
        out_specs=(anywhere, anywhere),
        scratch_shapes=[
            pltpu.SemaphoreType.DMA,
            pltpu.SemaphoreType.DMA((parts,)),
            pltpu.SemaphoreType.DMA((parts,)),
            pltpu.SemaphoreType.DMA((groups - 1,)),
            pltpu.SemaphoreType.DMA((groups - 1,)),
        ],
        compiler_params=pltpu.CompilerParams(collective_id=0, has_side_effects=True),
        name="spread",
    )(batch_rows.reshape(batch * 3, LANES), civec)

    vals, arows = pl.pallas_call(
        functools.partial(pick_kernel, parts, slots, batch),
        out_shape=(
            jax.ShapeDtypeStruct((batch, 3, slots_deep, LANES), F32),
            jax.ShapeDtypeStruct((ROWS, width), F32),
        ),
        in_specs=[smem, smem, smem, vmem, vmem, vmem, vmem, vmem],
        out_specs=(vmem, vmem),
        name="pick",
    )(mine[0].reshape(-1), mine[2].reshape(-1), local, code, table, civec, blocks, batch_rows)

    sigma, mixed, same = pl.pallas_call(
        functools.partial(reduce_kernel, groups, shape, slots, pairs),
        out_shape=(
            jax.ShapeDtypeStruct((batch, width), F32),
            jax.ShapeDtypeStruct((deep, 3 * LANES), F32),
            jax.ShapeDtypeStruct((deep, 3 * LANES), F32),
        ),
        in_specs=[vmem] * 8,
        out_specs=(vmem, vmem, vmem),
        scratch_shapes=[
            pltpu.VMEM((2, deep, width), F32),
            pltpu.VMEM((parts, per, 8, LANES), F32),
            pltpu.VMEM((parts, per, 8, LANES), F32),
            pltpu.VMEM((nz, per, 8, LANES), F32),
            pltpu.VMEM((groups, ny, nc, nz, per, 8, LANES), F32),
            pltpu.VMEM((groups * ROWS, 3 * LANES), F32),
            pltpu.SemaphoreType.DMA((parts,)),
            pltpu.SemaphoreType.DMA((parts,)),
            pltpu.SemaphoreType.DMA((nz,)),
            pltpu.SemaphoreType.DMA((nz,)),
            pltpu.SemaphoreType.DMA((groups, ny)),
            pltpu.SemaphoreType.DMA((groups, ny)),
            pltpu.SemaphoreType.DMA((groups, ny)),
            pltpu.SemaphoreType.DMA((groups, ny)),
        ],
        compiler_params=pltpu.CompilerParams(collective_id=1, has_side_effects=True),
        name="reduce",
    )(vals, code, arows, own_pair, pair_rows.reshape(1, groups * ROWS), ext, hpad[None], hpad[:, None])

    norm = total * width * parts
    root = math.sqrt(norm)
    density = jnp.stack([same[:pairs, pairs], mixed[pairs, :pairs]]) / root
    return sigma, density, same[:pairs, :pairs] / norm, mixed[:pairs, :pairs] / root


def solution(mesh, shape=(8, 4, 2)):
    in_specs = (P("alpha", "beta"), P(), P(), P(None, "beta", None), P())
    out_specs = (P("alpha", "beta"), P(), P(), P())
    return jax.shard_map(
        functools.partial(body, shape), mesh=mesh, in_specs=in_specs, out_specs=out_specs, check_vma=False
    )
```

time: 858 us -> 149 us (0.17); the launches traced: 846 us -> 148 us
  other arithmetic: 392 us -> 4.69 us
  waiting for transfers between devices: 179 us -> 0 us
  Pallas kernels: 0 us -> 128 us
  blocking collectives: 124 us -> 0 us
  local copies, waits for them, and re-layouts: 128 us -> 11.1 us
  between operations: 14.7 us -> 4.58 us
  matrix products: 9.02 us -> 0 us
    unnamed x6 -> x0, other arithmetic: 385 us -> none
    psum x1 -> x0, waiting for transfers between devices: 178 us -> none  [body(): lax.psum((totals[0], totals[1], totals[2]), ('alpha', 'beta'))]
    pallas_call x0 -> x3, Pallas kernels: none -> 128 us  [the longest x1 48.3 us: body(): pl.pallas_call(functools.partial(pick_kernel, parts, slots, batch), out_s...]
    gather x6 -> x0, local copies, waits for them, and re-layouts: 75.9 us -> none  [the longest x3 71.9 us: body(): beta_picked = spread[:, beta_sources]]
    psum x1 -> x0, blocking collectives: 75.3 us -> none  [body(): lax.psum((totals[0], totals[1], totals[2]), ('alpha', 'beta'))]
    all_gather x1 -> x0, blocking collectives: 48.8 us -> none  [body(): spread = lax.all_gather(batch_rows, 'beta', axis=1, tiled=True)]
    unnamed x11 -> x9, local copies, waits for them, and re-layouts: 35.6 us -> 0.6 us
    dot_general x6 -> x0, matrix products: 9.02 us -> none  [the longest x1 2.56 us: block_step(): mixed_part = jnp.einsum('bpn,bqn->pq', d_alpha, d_beta, precision=highest)]
  transfers between devices with their start and end apart: 2 -> 0, of which waited for: 1 -> 0; matrix products, arithmetic and copies ran while one was open for 61% -> 0% of each run, Pallas kernels for 0% -> 0%
where the time goes in v1:
time: 149 us; the launch traced here: 148 us
  Pallas kernels  128 us (86%)
  local copies, waits for them, and re-layouts  11.1 us (7%)
  other arithmetic  4.69 us (3%)
  between operations  4.58 us (3%)
    pallas_call x1, Pallas kernels, body(): pl.pallas_call(functools.partial(pick_kernel, parts, slots, batch), out_s...  48.3 us
    pallas_call x1, Pallas kernels, body(): pl.pallas_call(functools.partial(reduce_kernel, groups, shape, slots, pai...  45.3 us
    pallas_call x1, Pallas kernels, body(): pl.pallas_call(functools.partial(spread_kernel, groups, parts), out_shape...  34.2 us

profile of v1, /device:TPU:1, one launch (start us, length us, event | category | flops | bytes accessed | tf_op | source)
XLA Modules:
  0.0 148.2 jit_solution(12039961025141401836)
XLA Ops:
  0.6 0.7 dynamic-slice_subtract_fusion.local_ref
  1.4 0.6 fusion
  5.8 0.7 constant_dynamic-slice_fusion.3
  6.6 0.6 reshape.32.rows_ref
  7.2 34.2 %spread.1 = (f32[64,6,128]{2,1,0:T(8,128)}, f32[3,256,384]{2,1,0:T(8,128)}) custom-call(f32[6,128]{1,0:T(8,128)} %reshape.32.rows_ref, f32[256,384]{1,0:T(8,128)} %civ_ref.3), custom_call_target="tpu_custom_call" | custom-call | tf_op jit(solution)/shard_map/spread/pallas_call | solution.py:350
  41.5 0.7 constant_dynamic-slice_fusion.4
  42.2 0.6 reshape_squeeze.6.src_ref
  42.8 0.7 reshape_squeeze.7.sign_ref
  43.5 1.1 add_bitcast_fusion
  44.6 0.7 bitcast_bitcast_fusion.code_ref
  45.2 48.3 %pick.1 = (f32[2,3,88,128]{3,2,1,0:T(8,128)}, f32[168,384]{1,0:T(8,128)}) custom-call(s32[162]{0:T(256)} %reshape_squeeze.6.src_ref, s32[162]{0:T(256)} %reshape_squeeze.7.sign_ref, s32[2]{0:T(128)} %copy-done.1, s32[3,88,128]{2,1,0:T(8,128)} %bitcast_bitcast_fusion.code_ref, f32[64,6,128]{2,1,0:T(8,128)} %get-tuple-element.11.table_ref, ...), custom_call_target="tpu_custom_call" | custom-call | tf_op jit(solution)/shard_map/pick/pallas_call | solution.py:369
  93.5 0.7 slice_bitcast_fusion
  94.2 0.1 reshape.33
  94.3 0.6 constant_dynamic-slice_fusion.1.own_pair_ref
  95.0 0.6 reshape.35.ext_ref
  95.6 0.7 reshape.34.pair_ref
  96.2 0.8 broadcast_in_dim.8.hcol_ref
  97.0 0.6 broadcast_in_dim.6.hrow_ref
  97.6 45.3 %reduce.3 = (f32[2,384]{1,0:T(2,128)}, f32[328,384]{1,0:T(8,128)}, f32[328,384]{1,0:T(8,128)}) custom-call(f32[2,3,88,128]{3,2,1,0:T(8,128)} %get-tuple-element.13.vals_ref, s32[3,88,128]{2,1,0:T(8,128)} %bitcast_bitcast_fusion.code_ref, f32[168,384]{1,0:T(8,128)} %get-tuple-element.14.a_ref, s32[1,168]{1,0:T(1,128)} %constant_dynamic-slice_fusion.1.own_pair_ref, ...), custom_call_target="tpu_custom_call" | custom-call | tf_op jit(solution)/shard_map/reduce/pallas_call | solution.py:380
  142.9 2.2 %slice_multiply_fusion = (f32[324,324]{1,0:T(8,128)}, f32[324,324]{1,0:T(8,128)}) fusion(f32[328,384]{1,0:T(8,128)} %get-tuple-element.17, f32[328,384]{1,0:T(8,128)} %get-tuple-element.16), kind=kLoop, calls=%fused_computation | loop fusion | flops 209952 | bytes 1679616 | tf_op jit(solution)/shard_map/div | solution.py:412
  145.1 1.1 slice_reduce_fusion
  146.3 0.7 slice.50
  147.0 0.6 maximum_multiply_fusion
  147.6 0.6 copy.14
  (14 shorter events, 0.1 us)
Async XLA Ops:
  1.4 43.9 %copy-start.1 = (s32[2]{0:T(128)}, s32[2]{0:T(128)S(1)}, u32[]{:S(2)}) copy-start(s32[2]{0:T(128)S(1)} %dynamic-slice_subtract_fusion.local_ref) | copy-start | bytes 28
  6.6 38.7 %copy-start = (f32[2,384]{1,0:T(2,128)}, f32[2,384]{1,0:T(2,128)S(1)}, u32[]{:S(2)}) copy-start(f32[2,384]{1,0:T(2,128)S(1)} %pad_maximum_fusion.rows_ref) | copy-start | bytes 9220
  44.6 51.7 %copy-start.3 = (f32[324]{0:T(512)S(1)}, f32[324]{0:T(512)}, u32[]{:S(2)}) copy-start(f32[324]{0:T(512)} %param.9) | copy-start | bytes 3892
  142.9 4.7 %copy-start.2 = (f32[2,384]{1,0:T(2,128)S(1)}, f32[2,384]{1,0:T(2,128)}, u32[]{:S(2)}) copy-start(f32[2,384]{1,0:T(2,128)} %get-tuple-element.30) | copy-start | bytes 9220

commit v2 on v0

v2 whole, which is shorter than its diff:
```python
import functools
import math

import jax
import jax.numpy as jnp
from jax import lax
from jax.experimental import pallas as pl
from jax.experimental.pallas import tpu as pltpu
from jax.sharding import PartitionSpec as P

MESH = pl.DeviceIdType.MESH
F32, BF16, I32 = jnp.float32, jnp.bfloat16, jnp.int32
LANES = 128
HALF = 42
SHIFT = 68
ROWS = 168
EMPTY = 511
NT = (((1,), (1,)), ((), ()))
NN = (((1,), (0,)), ((), ()))
ALONG = lax.GatherDimensionNumbers(
    offset_dims=(), collapsed_slice_dims=(1,), start_index_map=(1,), operand_batching_dims=(0,), start_indices_batching_dims=(0,)
)


def split(x):
    high = x.astype(BF16)
    return high, (x - high.astype(F32)).astype(BF16)


def dot(a, b, dims):
    return lax.dot_general(a, b, dims, preferred_element_type=F32)


def dot3(a, b, dims):
    return dot(a[0], b[0], dims) + (dot(a[0], b[1], dims) + dot(a[1], b[0], dims))


def dot2(a, b, dims):
    return dot(a, b[0], dims) + dot(a, b[1], dims)


def lanes_of(x, index):
    return lax.gather(x, index[..., None], ALONG, (1, 1), mode=lax.GatherScatterMode.PROMISE_IN_BOUNDS)


def barrel(x, amount, bits):
    for bit in range(bits):
        moved = pltpu.roll(x, 1 << bit, 1)
        x = jnp.where(lax.rem(lax.div(amount, 1 << bit), 2) == 1, moved, x)
    return x


def packed_row(wide_ref, first, second, slots, end_first, end_second):
    string = slots + 1
    wide_ref[...] = jnp.zeros_like(wide_ref)
    wide_ref[0:1, 0:slots] = first
    wide_ref[1:2, 0:slots] = second
    lane = lax.broadcasted_iota(I32, (1, 2 * LANES), 1)
    blank = jnp.zeros((1, LANES), F32)
    one = jnp.concatenate([wide_ref[0:1, :], blank], axis=1)
    two = pltpu.roll(jnp.concatenate([wide_ref[1:2, :], blank], axis=1), string, 1)
    out = jnp.where(lane < string, one, two)
    out = jnp.where(lane == slots, end_first, jnp.where(lane == string + slots, end_second, out))
    return jnp.where(lane < 2 * string, out, float(EMPTY))


def main_kernel(groups, shape, slots, pairs, batch_ref, exc_ref, beta_ref, h_ref, civ_ref, sigma_ref, gat,
                code_n, code_ref, inv_ref, rows_s, table, texp, vals_ref, blk_ref, a_ref, wide_ref,
                tiles_ref, got_ref, zbuf,
                ts, tr, xs, xr, ssem, rsem, zs, zr, fs, fr, cs, cr):
    nz, ny, nc = shape
    parts = nz * ny * nc
    per = 64 // parts
    width = beta_ref.shape[1]
    cuts = width // LANES
    deep = 3 * LANES
    slots_deep = code_ref.shape[1]
    rows_dev = civ_ref.shape[0]
    string = slots + 1
    ga = lax.axis_index("alpha")
    me = lax.axis_index("beta")
    z, y, core = me // (ny * nc), (me // nc) % ny, me % nc
    planes = groups * ny

    def at(zz, yy, cc):
        return (zz * ny + yy) * nc + cc

    barrier = pltpu.get_barrier_semaphore()

    def greet(d, c):
        pl.semaphore_signal(barrier, inc=1, device_id=(ga, lax.rem(me + d, parts)), device_id_type=MESH)
        return c

    around = [(lax.rem(ga + k // ny, groups), lax.rem(y + k % ny, ny), k // ny) for k in range(1, planes)]
    extra = 0
    for aa, yy, off in around:
        if off:
            pl.semaphore_signal(barrier, inc=1, device_id=(aa, at(z, yy, core)), device_id_type=MESH)
            extra += 1
    lax.fori_loop(1, parts, greet, 0)

    for b in range(2):
        row = civ_ref[pl.ds(lax.rem(batch_ref[2 * ga + b], rows_dev), 1), :]
        for t in range(cuts):
            rows_s[b * cuts + t : b * cuts + t + 1, :] = row[:, t * LANES : (t + 1) * LANES]

    code_n[...] = jnp.full(code_n.shape, (EMPTY << 15) + (1 << 24), I32)
    code_n[:, 0:slots] = beta_ref[0] + beta_ref[1] * 32768 + (beta_ref[2] + 1) * (1 << 24)
    for lt in range(cuts):
        code_ref[lt] = code_n[lt * LANES : (lt + 1) * LANES, :].T[0:slots_deep]

    def invert(lt):
        for base in range(0, deep, LANES):
            ids = lax.broadcasted_iota(I32, (LANES, LANES), 0) + base

            def mark(e, acc):
                pair = jnp.bitwise_and(lax.shift_right_logical(code_ref[lt, pl.ds(e, 1), :], 15), 511)
                return jnp.where(pair == ids, e, acc)

            if base < pairs:
                acc = lax.fori_loop(0, slots, mark, jnp.full((LANES, LANES), LANES - 1, I32))
                inv_ref[lt * LANES : (lt + 1) * LANES, base : base + LANES] = acc.T

    for lt in range(cuts):
        invert(lt)

    pl.semaphore_wait(barrier, parts - 1 + extra)

    def row_copy(j, slot):
        return pltpu.make_async_remote_copy(
            rows_s, table.at[slot], ts.at[j], tr.at[slot], device_id=(ga, j), device_id_type=MESH
        )

    def send_row(d, c):
        row_copy(lax.rem(me + d, parts), me).start()
        return c

    lax.fori_loop(1, parts, send_row, 0)

    right, left = lax.rem(ga + 1, groups), lax.rem(ga + groups - 1, groups)
    half_rows = rows_dev // 2

    def block_copy(src, dst, k, to):
        return pltpu.make_async_remote_copy(
            src, dst, xs.at[k], xr.at[k], device_id=(to, me), device_id_type=MESH
        )

    first_half, second_half = pl.ds(0, half_rows), pl.ds(half_rows, half_rows)
    hops = [
        block_copy(civ_ref, blk_ref.at[0], 0, right),
        block_copy(civ_ref, blk_ref.at[1], 1, left),
        block_copy(blk_ref.at[0, first_half], blk_ref.at[2, first_half], 2, right),
        block_copy(blk_ref.at[1, second_half], blk_ref.at[2, second_half], 3, left),
    ]
    if groups == 2:
        hops = hops[:1]
    for hop in hops[:2]:
        hop.start()
    table[me] = rows_s[...]

    s_row = packed_row(
        wide_ref, exc_ref[0, pl.ds(2 * ga, 1), :].astype(F32), exc_ref[0, pl.ds(2 * ga + 1, 1), :].astype(F32), slots,
        batch_ref[2 * ga].astype(F32), batch_ref[2 * ga + 1].astype(F32),
    )
    g_row = packed_row(
        wide_ref, exc_ref[2, pl.ds(2 * ga, 1), :].astype(F32), exc_ref[2, pl.ds(2 * ga + 1, 1), :].astype(F32), slots, 1.0, 1.0
    )
    p_row = packed_row(
        wide_ref, exc_ref[1, pl.ds(2 * ga, 1), :].astype(F32), exc_ref[1, pl.ds(2 * ga + 1, 1), :].astype(F32), slots,
        float(pairs), float(pairs),
    )
    lane = lax.broadcasted_iota(I32, (1, 2 * LANES), 1)
    g_row = jnp.where(lane < 2 * string, g_row, 0.0)
    meta = jnp.concatenate([s_row, g_row, jnp.zeros((6, 2 * LANES), F32)], axis=0).T[0:ROWS]
    source, sign = meta[:, 0:1], meta[:, 1:2]

    def choose(block, owner):
        ids = (lax.broadcasted_iota(I32, (ROWS, rows_dev), 1) + owner * rows_dev).astype(F32)
        pick = jnp.where(source == ids, sign, 0.0).astype(BF16)
        parts2 = split(block)
        return dot(pick, parts2[0], NN), dot(pick, parts2[1], NN)

    a_high, a_low = choose(civ_ref[...], ga)

    def finish_row(d, c):
        j = lax.rem(me + d, parts)
        row_copy(j, j).wait_recv()
        return c

    lax.fori_loop(1, parts, finish_row, 0)

    def widen(j, c):
        for b in range(2):
            for t in range(cuts):
                texp[b, cuts * j + t] = jnp.broadcast_to(table[j, b * cuts + t : b * cuts + t + 1, :], (8, LANES))
        return c

    lax.fori_loop(0, parts, widen, 0)

    total_rows = parts * cuts
    chunk = 24 if total_rows % 24 == 0 else total_rows
    steps = chunk // 8 if chunk % 8 == 0 else 0

    def look_up(i, c):
        start = pl.multiple_of(8 * i, 8)
        for lt in range(cuts):
            code = code_ref[lt, pl.ds(start, 8), :]
            low = jnp.bitwise_and(code, 127)
            high = jnp.bitwise_and(lax.shift_right_logical(code, 7), 255)
            group = lax.shift_right_logical(high, 3)
            acc = [jnp.zeros((8, LANES), F32)] * 2
            index = jnp.broadcast_to(low[None], (chunk, 8, LANES)).reshape(chunk * 8, LANES)
            for base in range(0, total_rows, chunk):
                for b in range(2):
                    got = texp[b, base : base + chunk].reshape(chunk * 8, LANES)
                    got = lanes_of(got, index).reshape(chunk, 8, LANES)
                    for bit in range(3):
                        n = got.shape[0] // 2
                        got = got.reshape(n, 2, 8, LANES)
                        mask = jnp.broadcast_to(jnp.bitwise_and(high, 1 << bit)[None], (n, 8, LANES)) != 0
                        got = jnp.where(mask, got[:, 1], got[:, 0])
                    for k in range(steps):
                        acc[b] = jnp.where(group == base // 8 + k, got[k], acc[b])
            factor = (lax.shift_right_logical(code, 24) - 1).astype(F32)
            vals_ref[0, lt, pl.ds(start, 8), :] = acc[0] * factor
            vals_ref[1, lt, pl.ds(start, 8), :] = acc[1] * factor
        return c

    tiles = slots_deep // 8
    relay = tiles // 2
    lax.fori_loop(0, relay, look_up, 0)
    for hop in hops[:2]:
        hop.wait_recv()
    for hop in hops[2:]:
        hop.start()
    lax.fori_loop(relay, tiles, look_up, 0)

    blank = jnp.zeros((LANES - slots_deep, LANES), F32)
    d2 = []
    for b in range(2):
        by_slot = jnp.concatenate(
            [jnp.concatenate([vals_ref[b, lt], blank], axis=0).T for lt in range(cuts)], axis=0
        )
        d2.append(split(jnp.concatenate(
            [lanes_of(by_slot, inv_ref[:, base : base + LANES]) for base in range(0, deep, LANES)], axis=1
        )))

    for hop in hops[2:]:
        hop.wait_recv()
    owners = [lax.rem(ga + groups - 1, groups), lax.rem(ga + 1, groups), lax.rem(ga + 2, groups)]
    for k in range(groups - 1):
        more = choose(blk_ref[k], owners[k])
        a_high, a_low = a_high + more[0], a_low + more[1]
    a2 = (a_high.astype(BF16), a_low.astype(BF16))

    row = lax.broadcasted_iota(I32, (ROWS, 1), 0)
    first = row < string
    col_row = lax.broadcasted_iota(I32, (1, ROWS), 1)
    own = (lax.broadcasted_iota(I32, (deep, ROWS), 0).astype(F32) == p_row[:, 0:ROWS]).astype(BF16)
    wide_ref[...] = jnp.zeros_like(wide_ref)
    a_ref[...] = jnp.zeros_like(a_ref)
    a_ref[0:1, 0:pairs] = h_ref[...].reshape(1, pairs)
    hrow = split(jnp.broadcast_to(a_ref[0:1, :], (8, deep)))
    weight = dot(hrow[0], own, NN) + dot(hrow[1], own, NN)
    for b in range(2):
        part = jnp.where((col_row < string) == (b == 0), weight, 0.0)
        sigma_ref[b : b + 1, :] = (dot3(split(part), a2, NN) + dot3(hrow, d2[b], NT))[0:1]
    m = jnp.where(first, dot3(a2, d2[0], NN), dot3(a2, d2[1], NN))
    ext_i = lax.broadcasted_iota(I32, (LANES, ROWS), 0)
    ext_j = lax.broadcasted_iota(I32, (LANES, ROWS), 1)
    wrapped = jnp.where(ext_i >= string, ext_i - string, ext_i)
    grams = []
    for b in range(2):
        perm = (ext_j == wrapped + b * string).astype(BF16)
        ext = tuple(dot(perm, part, NN).astype(BF16) for part in a2)
        grams.append(dot3(a2, ext, NT))
    gram = jnp.where(first, grams[0], grams[1])
    local = jnp.where(first, row, row - string)
    folded = barrel(gram, lax.rem(SHIFT - local + 2 * LANES, LANES), 7)
    lane = lax.broadcasted_iota(I32, (ROWS, LANES), 1)
    last = jnp.where(lane < SHIFT, m[:, 2 * LANES :], jnp.where(lane < SHIFT + HALF, folded, 0.0))
    for rg in range(ROWS // 8):
        for lt in range(3):
            k = rg * 3 + lt
            piece = last if lt == 2 else m[:, lt * LANES : (lt + 1) * LANES]
            tiles_ref[k // per, k % per] = piece[8 * rg : 8 * rg + 8]
    tiles_ref[parts - 1, per - 1] = jnp.zeros((8, LANES), F32)

    def part_copy(j, slot):
        return pltpu.make_async_remote_copy(
            tiles_ref.at[j], got_ref.at[slot], ssem.at[j], rsem.at[slot], device_id=(ga, j), device_id_type=MESH
        )

    def send(d, c):
        part_copy(lax.rem(me + d, parts), me).start()
        return c

    lax.fori_loop(1, parts, send, 0)
    got_ref[me] = tiles_ref[me]

    def finish(d, c):
        j = lax.rem(me + d, parts)
        part_copy(j, j).wait_recv()
        return c

    lax.fori_loop(1, parts, finish, 0)
    zbuf[z] = jnp.sum(got_ref[...], axis=0)

    def z_copy(zz, slot):
        return pltpu.make_async_remote_copy(
            zbuf.at[slot], zbuf.at[slot], zs.at[zz], zr.at[slot], device_id=(ga, at(zz, y, core)), device_id_type=MESH
        )

    for k in range(1, nz):
        z_copy(lax.rem(z + k, nz), z).start()
    for k in range(1, nz):
        zz = lax.rem(z + k, nz)
        z_copy(zz, zz).wait_recv()

    def plane_copy(src, aa, yy, slot_a, slot_y):
        return pltpu.make_async_remote_copy(
            src, gat.at[slot_a, slot_y, core], fs.at[aa, yy], fr.at[slot_a, slot_y],
            device_id=(aa, at(z, yy, core)), device_id_type=MESH,
        )

    def twin_copy(src, slot_a, slot_y, slot_c):
        return pltpu.make_async_remote_copy(
            src, gat.at[slot_a, slot_y, slot_c], cs.at[slot_a, slot_y], cr.at[slot_a, slot_y],
            device_id=(ga, at(z, y, 1 - core)), device_id_type=MESH,
        )

    for aa, yy, _ in around:
        plane_copy(zbuf, aa, yy, ga, y).start()
    twin_copy(zbuf, ga, y, core).start()
    gat[ga, y, core] = zbuf[...]
    for aa, yy, _ in around:
        plane_copy(zbuf, aa, yy, aa, yy).wait_recv()
        twin_copy(gat.at[aa, yy, core], aa, yy, core).start()
    for aa, yy, _ in [(ga, y, 0)] + around:
        twin_copy(zbuf, aa, yy, 1 - core).wait_recv()

    def drain(d, c):
        j = lax.rem(me + d, parts)
        part_copy(j, j).wait_send()
        row_copy(j, j).wait_send()
        return c

    lax.fori_loop(1, parts, drain, 0)
    for hop in hops:
        hop.wait_send()
    for k in range(1, nz):
        z_copy(lax.rem(z + k, nz), z).wait_send()
    for aa, yy, _ in around:
        plane_copy(zbuf, aa, yy, ga, y).wait_send()
    for aa, yy, _ in [(ga, y, 0)] + around:
        twin_copy(zbuf, aa, yy, core).wait_send()


def place_kernel(groups, shape, slots, pairs, norm, exc_ref, gat, sigma_in, sigma_ref, density_ref, same_ref, mixed_ref,
                 r_ref, wide_ref):
    nz, ny, nc = shape
    per = 64 // (nz * ny * nc)
    string = slots + 1
    deep = 3 * LANES
    sigma_ref[...] = sigma_in[...]
    row = lax.broadcasted_iota(I32, (ROWS, 1), 0)
    first = row < string
    local = jnp.where(first, row, row - string)
    amount = lax.rem(local - SHIFT + 2 * LANES, LANES)
    lane = lax.broadcasted_iota(I32, (ROWS, LANES), 1)
    weights = jnp.where((lane == SHIFT) | (lane == SHIFT + HALF - 1), 0.5, 1.0)
    weights = jnp.where((lane >= SHIFT) & (lane < SHIFT + HALF), weights, 0.0)
    strip = lax.broadcasted_iota(I32, (1, LANES), 1)
    mixed = jnp.zeros((deep, deep), F32)
    upper = jnp.zeros((deep, deep), F32)
    for g in range(groups):
        for rg in range(ROWS // 8):
            for lt in range(3):
                k = rg * 3 + lt
                j, s = k // per, k % per
                r_ref[8 * rg : 8 * rg + 8, lt * LANES : (lt + 1) * LANES] = gat[
                    g, (j // nc) % ny, j % nc, j // (ny * nc), s
                ]
        ids = exc_ref[1, 2 * g : 2 * g + 2, :].astype(F32)
        p_row = packed_row(wide_ref, ids[0:1], ids[1:2], slots, float(pairs), float(pairs))
        placing = (lax.broadcasted_iota(I32, (deep, ROWS), 0).astype(F32) == p_row[:, 0:ROWS]).astype(BF16)
        mixed = mixed + dot2(placing, split(r_ref[...]), NN)
        half = barrel(r_ref[:, 2 * LANES :] * weights, amount, 7)
        both = jnp.concatenate([jnp.where(first, half, 0.0), jnp.where(first, 0.0, half)], axis=1)
        ends = []
        for b in range(2):
            line = wide_ref[b : b + 1, :]
            again = pltpu.roll(line, string, 1)
            line = jnp.where(strip < slots, line, jnp.where(strip == slots, float(pairs), again))
            ends.append(line)
        ext = jnp.concatenate(ends, axis=1)
        right = (lax.broadcasted_iota(I32, (deep, 2 * LANES), 0).astype(F32) == ext).astype(BF16)
        t = sum(dot(p, right, NT) for p in split(both))
        upper = upper + dot2(placing, split(t), NN)
    root = math.sqrt(norm)
    same = upper + upper.T
    density_ref[0:1, :] = same[pairs : pairs + 1, 0:pairs] * (1.0 / root)
    density_ref[1:2, :] = mixed[pairs : pairs + 1, 0:pairs] * (1.0 / root)
    same_ref[...] = same[0:pairs, 0:pairs] * (1.0 / norm)
    mixed_ref[...] = mixed[0:pairs, 0:pairs] * (1.0 / root)


def body(shape, civec, batch_index, exc_alpha, exc_beta, one_body):
    vmem = pl.BlockSpec(memory_space=pltpu.VMEM)
    smem = pl.BlockSpec(memory_space=pltpu.SMEM)
    nz, ny, nc = shape
    parts = nz * ny * nc
    per = 64 // parts
    groups = lax.axis_size("alpha")
    rows_dev, width = civec.shape
    total = batch_index.shape[0]
    batch = total // groups
    slots = exc_alpha.shape[2]
    pairs = one_body.shape[0]
    deep = 3 * LANES
    cuts = width // LANES
    slots_deep = -(-slots // 8) * 8
    dma = pltpu.SemaphoreType.DMA
    sigma, gat = pl.pallas_call(
        functools.partial(main_kernel, groups, shape, slots, pairs),
        out_shape=(
            jax.ShapeDtypeStruct((batch, width), F32),
            jax.ShapeDtypeStruct((groups, ny, nc, nz, per, 8, LANES), F32),
        ),
        in_specs=[smem, vmem, vmem, vmem, vmem],
        out_specs=(vmem, vmem),
        scratch_shapes=[
            pltpu.VMEM((width, LANES), I32),
            pltpu.VMEM((cuts, slots_deep, LANES), I32),
            pltpu.VMEM((width, deep), I32),
            pltpu.VMEM((2 * cuts, LANES), F32),
            pltpu.VMEM((parts, 2 * cuts, LANES), F32),
            pltpu.VMEM((2, parts * cuts, 8, LANES), F32),
            pltpu.VMEM((2, cuts, slots_deep, LANES), F32),
            pltpu.VMEM((max(groups - 1, 2), rows_dev, width), F32),
            pltpu.VMEM((8, deep), F32),
            pltpu.VMEM((8, LANES), F32),
            pltpu.VMEM((parts, per, 8, LANES), F32),
            pltpu.VMEM((parts, per, 8, LANES), F32),
            pltpu.VMEM((nz, per, 8, LANES), F32),
            dma((parts,)), dma((parts,)),
            dma((4,)), dma((4,)),
            dma((parts,)), dma((parts,)),
            dma((nz,)), dma((nz,)),
            dma((groups, ny)), dma((groups, ny)),
            dma((groups, ny)), dma((groups, ny)),
        ],
        compiler_params=pltpu.CompilerParams(collective_id=0, has_side_effects=True),
        name="main",
    )(batch_index, exc_alpha, exc_beta, one_body, civec)
    return tuple(pl.pallas_call(
        functools.partial(place_kernel, groups, shape, slots, pairs, total * width * parts),
        out_shape=(
            jax.ShapeDtypeStruct((batch, width), F32),
            jax.ShapeDtypeStruct((2, pairs), F32),
            jax.ShapeDtypeStruct((pairs, pairs), F32),
            jax.ShapeDtypeStruct((pairs, pairs), F32),
        ),
        in_specs=[vmem, vmem, vmem],
        out_specs=(vmem, vmem, vmem, vmem),
        scratch_shapes=[pltpu.VMEM((ROWS, deep), F32), pltpu.VMEM((8, LANES), F32)],
        name="place",
    )(exc_alpha, gat, sigma))


def solution(mesh, shape=(8, 4, 2)):
    in_specs = (P("alpha", "beta"), P(), P(), P(None, "beta", None), P())
    out_specs = (P("alpha", "beta"), P(), P(), P())
    return jax.shard_map(
        functools.partial(body, shape), mesh=mesh, in_specs=in_specs, out_specs=out_specs, check_vma=False
    )
```

time: 858 us -> 85.9 us (0.10); the launches traced: 846 us -> 85.7 us
  other arithmetic: 392 us -> 0 us
  waiting for transfers between devices: 179 us -> 0 us
  local copies, waits for them, and re-layouts: 128 us -> 2.08 us
  blocking collectives: 124 us -> 0 us
  Pallas kernels: 0 us -> 83 us
  between operations: 14.7 us -> 0.64 us
  matrix products: 9.02 us -> 0 us
    unnamed x6 -> x0, other arithmetic: 385 us -> none
    psum x1 -> x0, waiting for transfers between devices: 178 us -> none  [body(): lax.psum((totals[0], totals[1], totals[2]), ('alpha', 'beta'))]
    pallas_call x0 -> x2, Pallas kernels: none -> 83 us  [the longest x1 77.7 us: body(): pl.pallas_call(functools.partial(main_kernel, groups, shape, slots, pairs...]
    gather x6 -> x0, local copies, waits for them, and re-layouts: 75.9 us -> none  [the longest x3 71.9 us: body(): beta_picked = spread[:, beta_sources]]
    psum x1 -> x0, blocking collectives: 75.3 us -> none  [body(): lax.psum((totals[0], totals[1], totals[2]), ('alpha', 'beta'))]
    all_gather x1 -> x0, blocking collectives: 48.8 us -> none  [body(): spread = lax.all_gather(batch_rows, 'beta', axis=1, tiled=True)]
    unnamed x11 -> x1, local copies, waits for them, and re-layouts: 35.6 us -> 2.08 us
    dot_general x6 -> x0, matrix products: 9.02 us -> none  [the longest x1 2.56 us: block_step(): mixed_part = jnp.einsum('bpn,bqn->pq', d_alpha, d_beta, precision=highest)]
  transfers between devices with their start and end apart: 2 -> 0, of which waited for: 1 -> 0; matrix products, arithmetic and copies ran while one was open for 61% -> 0% of each run, Pallas kernels for 0% -> 0%
where the time goes in v2:
time: 85.9 us; the launch traced here: 85.7 us
  Pallas kernels  83 us (97%)
  local copies, waits for them, and re-layouts  2.08 us (2%)
    pallas_call x1, Pallas kernels, body(): pl.pallas_call(functools.partial(main_kernel, groups, shape, slots, pairs...  77.7 us
    pallas_call x1, Pallas kernels, body(): pl.pallas_call(functools.partial(place_kernel, groups, shape, slots, pair...  5.31 us
    unnamed x1, local copies, waits for them, and re-layouts  2.08 us

profile of v2, /device:TPU:1, one launch (start us, length us, event | category | flops | bytes accessed | tf_op | source)
XLA Modules:
  0.0 85.7 jit_solution(4948677903729209227)
XLA Ops:
  0.6 2.1 %copy.9.beta_ref = s32[3,384,81]{2,1,0:T(8,128)} copy(s32[3,384,81]{1,2,0:T(8,128)} %param.8) | data formatting | bytes 746496 | tf_op args[3]
  2.7 77.7 %main.1 = (f32[2,384]{1,0:T(2,128)}, f32[4,4,2,8,1,8,128]{6,5,4,3,2,1,0:T(8,128)}) custom-call(s32[8]{0:T(128)} %batch_ref.1, s32[3,8,81]{2,1,0:T(8,128)} %exc_ref.3, s32[3,384,81]{2,1,0:T(8,128)} %copy.9.beta_ref, f32[324]{0:T(512)} %h_ref.1, f32[256,384]{1,0:T(8,128)} %civ_ref.1), custom_call_target="tpu_custom_call" | custom-call | tf_op jit(solution)/shard_map/main/pallas_call | solution.py:424
  80.4 5.3 %place.1 = (f32[2,384]{1,0:T(2,128)}, f32[2,324]{1,0:T(2,128)}, f32[324,324]{1,0:T(8,128)}, f32[324,324]{1,0:T(8,128)}) custom-call(s32[3,8,81]{2,1,0:T(8,128)} %exc_ref.3, f32[4,4,2,8,1,8,128]{6,5,4,3,2,1,0:T(8,128)} %get-tuple-element.6.gat, f32[2,384]{1,0:T(2,128)} %get-tuple-element.7.sigma_in), custom_call_target="tpu_custom_call" | custom-call | tf_op jit(solution)/shard_map/place/pallas_call | solution.py:456

commit v3 on v2

--- a/solution.py
+++ b/solution.py
@@ -65,16 +65,16 @@
 
 
 def main_kernel(groups, shape, slots, pairs, batch_ref, exc_ref, beta_ref, h_ref, civ_ref, sigma_ref, gat,
-                code_n, code_ref, inv_ref, rows_s, table, texp, vals_ref, blk_ref, a_ref, wide_ref,
-                tiles_ref, got_ref, zbuf,
+                pair_ref, look_ref, sign_ref, hx_ref, inv_ref, rows_s, table, texp, t_ref, vals_ref, blk_ref, line_ref,
+                wide_ref, tiles_ref, got_ref, zbuf,
                 ts, tr, xs, xr, ssem, rsem, zs, zr, fs, fr, cs, cr):
     nz, ny, nc = shape
     parts = nz * ny * nc
     per = 64 // parts
-    width = beta_ref.shape[1]
+    width = beta_ref.shape[2]
     cuts = width // LANES
     deep = 3 * LANES
-    slots_deep = code_ref.shape[1]
+    slots_deep = look_ref.shape[1]
     rows_dev = civ_ref.shape[0]
     string = slots + 1
     ga = lax.axis_index("alpha")
@@ -104,25 +104,35 @@
         for t in range(cuts):
             rows_s[b * cuts + t : b * cuts + t + 1, :] = row[:, t * LANES : (t + 1) * LANES]
 
-    code_n[...] = jnp.full(code_n.shape, (EMPTY << 15) + (1 << 24), I32)
-    code_n[:, 0:slots] = beta_ref[0] + beta_ref[1] * 32768 + (beta_ref[2] + 1) * (1 << 24)
+    last_tile = slots_deep - 8
     for lt in range(cuts):
-        code_ref[lt] = code_n[lt * LANES : (lt + 1) * LANES, :].T[0:slots_deep]
-
-    def invert(lt):
-        for base in range(0, deep, LANES):
-            ids = lax.broadcasted_iota(I32, (LANES, LANES), 0) + base
-
-            def mark(e, acc):
-                pair = jnp.bitwise_and(lax.shift_right_logical(code_ref[lt, pl.ds(e, 1), :], 15), 511)
-                return jnp.where(pair == ids, e, acc)
-
-            if base < pairs:
-                acc = lax.fori_loop(0, slots, mark, jnp.full((LANES, LANES), LANES - 1, I32))
-                inv_ref[lt * LANES : (lt + 1) * LANES, base : base + LANES] = acc.T
-
-    for lt in range(cuts):
-        invert(lt)
+        cut = slice(lt * LANES, (lt + 1) * LANES)
+        pair_ref[lt, last_tile:, :] = jnp.full((8, LANES), EMPTY, I32)
+        look_ref[lt, last_tile:, :] = jnp.zeros((8, LANES), I32)
+        sign_ref[lt, last_tile:, :] = jnp.zeros((8, LANES), F32)
+        look_ref[lt, 0:slots, :] = beta_ref[0, :, cut]
+        pair_ref[lt, 0:slots, :] = beta_ref[1, :, cut]
+        sign_ref[lt, 0:slots, :] = beta_ref[2, :, cut].astype(F32)
+
+    blocks = [(lt, base) for base in range(0, pairs, LANES) for lt in range(cuts)]
+
+    def invert(lt, base):
+        size = min(LANES, -(-(pairs - base) // 8) * 8)
+        ids = lax.broadcasted_iota(I32, (size, LANES), 0) + base
+
+        def mark(e, acc):
+            for k in range(9):
+                acc = jnp.where(pair_ref[lt, pl.ds(9 * e + k, 1), :] == ids, 9 * e + k, acc)
+            return acc
+
+        acc = lax.fori_loop(0, slots // 9, mark, jnp.full((size, LANES), LANES - 1, I32))
+        if size < LANES:
+            acc = jnp.concatenate([acc, jnp.full((LANES - size, LANES), LANES - 1, I32)], axis=0)
+        inv_ref[lt * LANES : (lt + 1) * LANES, base : base + LANES] = acc.T
+
+    early = len(blocks) // 2
+    for block in blocks[:early]:
+        invert(*block)
 
     pl.semaphore_wait(barrier, parts - 1 + extra)
 
@@ -158,6 +168,29 @@
         hop.start()
     table[me] = rows_s[...]
 
+    for block in blocks[early:]:
+        invert(*block)
+
+    line_ref[...] = jnp.zeros_like(line_ref)
+    line_ref[0:1, 0:pairs] = h_ref[...].reshape(1, pairs)
+    strips = [jnp.broadcast_to(line_ref[0:1, k * LANES : (k + 1) * LANES], (8, LANES)) for k in range(3)]
+
+    def h_of(index):
+        low = jnp.bitwise_and(index, 127)
+        high = lax.shift_right_logical(index, 7)
+        out = jnp.zeros(index.shape, F32)
+        for k in range(3):
+            out = jnp.where(high == k, lanes_of(strips[k], low), out)
+        return out
+
+    def h_step(i, c):
+        start = pl.multiple_of(8 * i, 8)
+        for lt in range(cuts):
+            hx_ref[lt, pl.ds(start, 8), :] = h_of(pair_ref[lt, pl.ds(start, 8), :])
+        return c
+
+    lax.fori_loop(0, slots_deep // 8, h_step, 0)
+
     s_row = packed_row(
         wide_ref, exc_ref[0, pl.ds(2 * ga, 1), :].astype(F32), exc_ref[0, pl.ds(2 * ga + 1, 1), :].astype(F32), slots,
         batch_ref[2 * ga].astype(F32), batch_ref[2 * ga + 1].astype(F32),
@@ -167,11 +200,17 @@
     )
     p_row = packed_row(
         wide_ref, exc_ref[1, pl.ds(2 * ga, 1), :].astype(F32), exc_ref[1, pl.ds(2 * ga + 1, 1), :].astype(F32), slots,
-        float(pairs), float(pairs),
+        float(EMPTY), float(EMPTY),
     )
-    lane = lax.broadcasted_iota(I32, (1, 2 * LANES), 1)
-    g_row = jnp.where(lane < 2 * string, g_row, 0.0)
-    meta = jnp.concatenate([s_row, g_row, jnp.zeros((6, 2 * LANES), F32)], axis=0).T[0:ROWS]
+    wide_lane = lax.broadcasted_iota(I32, (1, 2 * LANES), 1)
+    g_row = jnp.where(wide_lane < 2 * string, g_row, 0.0)
+    h_row = jnp.concatenate(
+        [h_of(jnp.broadcast_to(p_row[:, k : k + LANES], (8, LANES)).astype(I32))[0:1] for k in (0, LANES)], axis=1
+    )
+    meta = jnp.concatenate(
+        [s_row, g_row, jnp.where(wide_lane < string, h_row, 0.0), jnp.where(wide_lane < string, 0.0, h_row),
+         jnp.zeros((4, 2 * LANES), F32)], axis=0
+    ).T[0:ROWS]
     source, sign = meta[:, 0:1], meta[:, 1:2]
 
     def choose(block, owner):
@@ -182,46 +221,73 @@
 
     a_high, a_low = choose(civ_ref[...], ga)
 
+    def arrive(j):
+        for b in range(2):
+            for t in range(cuts):
+                line = table[j, b * cuts + t : b * cuts + t + 1, :]
+                texp[b, cuts * j + t] = jnp.broadcast_to(line, (8, LANES))
+                t_ref[b, pl.ds(cuts * j + t, 1), :] = line
+
     def finish_row(d, c):
         j = lax.rem(me + d, parts)
         row_copy(j, j).wait_recv()
-        return c
-
+        arrive(j)
+        return c
+
+    arrive(me)
     lax.fori_loop(1, parts, finish_row, 0)
 
-    def widen(j, c):
-        for b in range(2):
-            for t in range(cuts):
-                texp[b, cuts * j + t] = jnp.broadcast_to(table[j, b * cuts + t : b * cuts + t + 1, :], (8, LANES))
-        return c
-
-    lax.fori_loop(0, parts, widen, 0)
-
     total_rows = parts * cuts
-    chunk = 24 if total_rows % 24 == 0 else total_rows
-    steps = chunk // 8 if chunk % 8 == 0 else 0
+    chunk = 24
+    halves = split(jnp.concatenate([t_ref[0], t_ref[1]], axis=0))
+    full = jnp.concatenate(halves, axis=1)
+
+    def mux(got, high):
+        for bit in range(3):
+            n = got.shape[0] // 2
+            got = got.reshape(n, 2, 8, LANES)
+            mask = jnp.broadcast_to(jnp.bitwise_and(high, 1 << bit)[None], (n, 8, LANES)) != 0
+            got = jnp.where(mask, got[:, 1], got[:, 0])
+        return got
+
+    sub = lax.broadcasted_iota(I32, (8, LANES), 0)
+    tall = lax.broadcasted_iota(I32, (LANES, LANES), 0)
 
     def look_up(i, c):
         start = pl.multiple_of(8 * i, 8)
         for lt in range(cuts):
-            code = code_ref[lt, pl.ds(start, 8), :]
-            low = jnp.bitwise_and(code, 127)
-            high = jnp.bitwise_and(lax.shift_right_logical(code, 7), 255)
-            group = lax.shift_right_logical(high, 3)
+            src = look_ref[lt, pl.ds(start, 8), :]
+            low = jnp.bitwise_and(src, 127)
+            high = lax.shift_right_logical(src, 7)
             acc = [jnp.zeros((8, LANES), F32)] * 2
-            index = jnp.broadcast_to(low[None], (chunk, 8, LANES)).reshape(chunk * 8, LANES)
-            for base in range(0, total_rows, chunk):
-                for b in range(2):
-                    got = texp[b, base : base + chunk].reshape(chunk * 8, LANES)
-                    got = lanes_of(got, index).reshape(chunk, 8, LANES)
-                    for bit in range(3):
-                        n = got.shape[0] // 2
-                        got = got.reshape(n, 2, 8, LANES)
-                        mask = jnp.broadcast_to(jnp.bitwise_and(high, 1 << bit)[None], (n, 8, LANES)) != 0
-                        got = jnp.where(mask, got[:, 1], got[:, 0])
-                    for k in range(steps):
-                        acc[b] = jnp.where(group == base // 8 + k, got[k], acc[b])
-            factor = (lax.shift_right_logical(code, 24) - 1).astype(F32)
+            if lt == 0:
+                group = lax.shift_right_logical(high, 3)
+                index = jnp.broadcast_to(low[None], (chunk, 8, LANES)).reshape(chunk * 8, LANES)
+                for base in range(0, total_rows, chunk):
+                    for b in range(2):
+                        got = texp[b, base : base + chunk].reshape(chunk * 8, LANES)
+                        got = mux(lanes_of(got, index).reshape(chunk, 8, LANES), high)
+                        for k in range(chunk // 8):
+                            acc[b] = jnp.where(group == base // 8 + k, got[k], acc[b])
+            else:
+                for r in range(0, 8, 2):
+                    hot = jnp.concatenate(
+                        [(tall == low[r + k : r + k + 1]).astype(F32).astype(BF16) for k in range(2)], axis=1
+                    )
+                    found = dot(full, jnp.concatenate([hot, hot], axis=0), NN)
+                    for k in range(2):
+                        wide = jnp.broadcast_to(high[r + k : r + k + 1], (8, LANES))
+                        near = jnp.bitwise_and(wide, 7) == sub
+                        group = lax.shift_right_logical(wide, 3)
+                        for b in range(2):
+                            mine = found[b * total_rows : (b + 1) * total_rows, k * LANES : (k + 1) * LANES]
+                            mine = mine.reshape(total_rows // 8, 8, LANES)
+                            best = mine[0]
+                            for q in range(1, total_rows // 8):
+                                best = jnp.where(group == q, mine[q], best)
+                            value = jnp.sum(jnp.where(near, best, 0.0), axis=0, keepdims=True)
+                            acc[b] = jnp.where(sub == r + k, value, acc[b])
+            factor = sign_ref[lt, pl.ds(start, 8), :]
             vals_ref[0, lt, pl.ds(start, 8), :] = acc[0] * factor
             vals_ref[1, lt, pl.ds(start, 8), :] = acc[1] * factor
         return c
@@ -252,32 +318,38 @@
         more = choose(blk_ref[k], owners[k])
         a_high, a_low = a_high + more[0], a_low + more[1]
     a2 = (a_high.astype(BF16), a_low.astype(BF16))
+    a = a_high + a_low
+
+    for b in range(2):
+        from_a = jnp.sum(a * meta[:, 2 + b : 3 + b], axis=0, keepdims=True)
+        for lt in range(cuts):
+            cut = slice(lt * LANES, (lt + 1) * LANES)
+            from_b = jnp.sum(vals_ref[b, lt] * hx_ref[lt], axis=0, keepdims=True)
+            sigma_ref[b : b + 1, cut] = from_a[:, cut] + from_b
+
+    def times(left, right, dims):
+        n = left[0].shape[0]
+        both = dot(jnp.concatenate(left, axis=0), right[0], dims)
+        return (both[:n] + both[n:]) + dot(left[0], right[1], dims)
 
     row = lax.broadcasted_iota(I32, (ROWS, 1), 0)
     first = row < string
-    col_row = lax.broadcasted_iota(I32, (1, ROWS), 1)
-    own = (lax.broadcasted_iota(I32, (deep, ROWS), 0).astype(F32) == p_row[:, 0:ROWS]).astype(BF16)
-    wide_ref[...] = jnp.zeros_like(wide_ref)
-    a_ref[...] = jnp.zeros_like(a_ref)
-    a_ref[0:1, 0:pairs] = h_ref[...].reshape(1, pairs)
-    hrow = split(jnp.broadcast_to(a_ref[0:1, :], (8, deep)))
-    weight = dot(hrow[0], own, NN) + dot(hrow[1], own, NN)
-    for b in range(2):
-        part = jnp.where((col_row < string) == (b == 0), weight, 0.0)
-        sigma_ref[b : b + 1, :] = (dot3(split(part), a2, NN) + dot3(hrow, d2[b], NT))[0:1]
-    m = jnp.where(first, dot3(a2, d2[0], NN), dot3(a2, d2[1], NN))
-    ext_i = lax.broadcasted_iota(I32, (LANES, ROWS), 0)
-    ext_j = lax.broadcasted_iota(I32, (LANES, ROWS), 1)
-    wrapped = jnp.where(ext_i >= string, ext_i - string, ext_i)
-    grams = []
-    for b in range(2):
-        perm = (ext_j == wrapped + b * string).astype(BF16)
-        ext = tuple(dot(perm, part, NN).astype(BF16) for part in a2)
-        grams.append(dot3(a2, ext, NT))
-    gram = jnp.where(first, grams[0], grams[1])
+    low_rows, high_rows = 96, 80
+    m0 = times(tuple(p[:low_rows] for p in a2), d2[0], NN)
+    m1 = times(tuple(p[high_rows:] for p in a2), d2[1], NN)
+    m = jnp.where(
+        first,
+        jnp.concatenate([m0, jnp.zeros((ROWS - low_rows, deep), F32)], axis=0),
+        jnp.concatenate([jnp.zeros((high_rows, deep), F32), m1], axis=0),
+    )
+    gram = times(a2, a2, NT)
+    gram = jnp.concatenate([gram, jnp.zeros((ROWS, 2 * LANES - ROWS), F32)], axis=1)
+    gram = jnp.where(first, gram, pltpu.roll(gram, 2 * LANES - string, 1))
+    again = pltpu.roll(gram, string, 1)[:, 0:LANES]
+    lane = lax.broadcasted_iota(I32, (ROWS, LANES), 1)
+    gram = jnp.where(lane < string, gram[:, 0:LANES], again)
     local = jnp.where(first, row, row - string)
     folded = barrel(gram, lax.rem(SHIFT - local + 2 * LANES, LANES), 7)
-    lane = lax.broadcasted_iota(I32, (ROWS, LANES), 1)
     last = jnp.where(lane < SHIFT, m[:, 2 * LANES :], jnp.where(lane < SHIFT + HALF, folded, 0.0))
     for rg in range(ROWS // 8):
         for lt in range(3):
@@ -430,12 +502,15 @@
         in_specs=[smem, vmem, vmem, vmem, vmem],
         out_specs=(vmem, vmem),
         scratch_shapes=[
-            pltpu.VMEM((width, LANES), I32),
             pltpu.VMEM((cuts, slots_deep, LANES), I32),
+            pltpu.VMEM((cuts, slots_deep, LANES), I32),
+            pltpu.VMEM((cuts, slots_deep, LANES), F32),
+            pltpu.VMEM((cuts, slots_deep, LANES), F32),
             pltpu.VMEM((width, deep), I32),
             pltpu.VMEM((2 * cuts, LANES), F32),
             pltpu.VMEM((parts, 2 * cuts, LANES), F32),
             pltpu.VMEM((2, parts * cuts, 8, LANES), F32),
+            pltpu.VMEM((2, parts * cuts, LANES), F32),
             pltpu.VMEM((2, cuts, slots_deep, LANES), F32),
             pltpu.VMEM((max(groups - 1, 2), rows_dev, width), F32),
             pltpu.VMEM((8, deep), F32),
@@ -452,7 +527,7 @@
         ],
         compiler_params=pltpu.CompilerParams(collective_id=0, has_side_effects=True),
         name="main",
-    )(batch_index, exc_alpha, exc_beta, one_body, civec)
+    )(batch_index, exc_alpha, exc_beta.swapaxes(1, 2), one_body, civec)
     return tuple(pl.pallas_call(
         functools.partial(place_kernel, groups, shape, slots, pairs, total * width * parts),
         out_shape=(

time: 85.9 us -> 68.6 us (0.80)
  Pallas kernels: 83 us -> 67.8 us
  local copies, waits for them, and re-layouts: 2.08 us -> 0 us
    pallas_call x1, Pallas kernels: 77.7 us -> 62.5 us  [body(): pl.pallas_call(functools.partial(main_kernel, groups, shape, slots, pairs...]
    unnamed x1 -> x0, local copies, waits for them, and re-layouts: 2.08 us -> none
where the time goes in v3:
time: 68.6 us; the launch traced here: 68.4 us
  Pallas kernels  67.8 us (99%)
    pallas_call x1, Pallas kernels, body(): pl.pallas_call(functools.partial(main_kernel, groups, shape, slots, pairs...  62.5 us
    pallas_call x1, Pallas kernels, body(): pl.pallas_call(functools.partial(place_kernel, groups, shape, slots, pair...  5.3 us

profile of v3, /device:TPU:1, one launch (start us, length us, event | category | flops | bytes accessed | tf_op | source)
XLA Modules:
  0.0 68.4 jit_solution(6650001223633023021)
XLA Ops:
  0.6 62.5 %main.1 = (f32[2,384]{1,0:T(2,128)}, f32[4,4,2,8,1,8,128]{6,5,4,3,2,1,0:T(8,128)}) custom-call(s32[8]{0:T(128)} %batch_ref.1, s32[3,8,81]{2,1,0:T(8,128)} %exc_ref.3, s32[3,81,384]{2,1,0:T(8,128)} %bitcast.1, f32[324]{0:T(512)} %h_ref.1, f32[256,384]{1,0:T(8,128)} %civ_ref.1), custom_call_target="tpu_custom_call" | custom-call | tf_op jit(solution)/shard_map/main/pallas_call | solution.py:496
  63.1 5.3 %place.1 = (f32[2,384]{1,0:T(2,128)}, f32[2,324]{1,0:T(2,128)}, f32[324,324]{1,0:T(8,128)}, f32[324,324]{1,0:T(8,128)}) custom-call(s32[3,8,81]{2,1,0:T(8,128)} %exc_ref.3, f32[4,4,2,8,1,8,128]{6,5,4,3,2,1,0:T(8,128)} %get-tuple-element.6.gat, f32[2,384]{1,0:T(2,128)} %get-tuple-element.7.sigma_in), custom_call_target="tpu_custom_call" | custom-call | tf_op jit(solution)/shard_map/place/pallas_call | solution.py:531

commit v4 on v3

--- a/solution.py
+++ b/solution.py
@@ -66,8 +66,8 @@
 
 def main_kernel(groups, shape, slots, pairs, batch_ref, exc_ref, beta_ref, h_ref, civ_ref, sigma_ref, gat,
                 pair_ref, look_ref, sign_ref, hx_ref, inv_ref, rows_s, table, texp, t_ref, vals_ref, blk_ref, line_ref,
-                wide_ref, tiles_ref, got_ref, zbuf,
-                ts, tr, xs, xr, ssem, rsem, zs, zr, fs, fr, cs, cr):
+                wide_ref, tiles_ref, pair_buf, sums, got_ref, zbuf, dummy,
+                ts, tr, xs, xr, ps, pr, ssem, rsem, zs, zr, fs, fr, cs, cr):
     nz, ny, nc = shape
     parts = nz * ny * nc
     per = 64 // parts
@@ -86,19 +86,32 @@
         return (zz * ny + yy) * nc + cc
 
     barrier = pltpu.get_barrier_semaphore()
-
-    def greet(d, c):
-        pl.semaphore_signal(barrier, inc=1, device_id=(ga, lax.rem(me + d, parts)), device_id_type=MESH)
-        return c
-
-    around = [(lax.rem(ga + k // ny, groups), lax.rem(y + k % ny, ny), k // ny) for k in range(1, planes)]
+    others = parts - 1
+    burst = 7 if others % 7 == 0 else 1
+
+    def far_first(k):
+        return lax.rem(me + 1 + lax.rem(k + (others * 5) // 16, others), parts)
+
+    def each(action):
+        def step(k, c):
+            for i in range(burst):
+                action(far_first(burst * k + i))
+            return c
+
+        lax.fori_loop(0, others // burst, step, 0)
+
+    each(lambda j: pl.semaphore_signal(barrier, inc=1, device_id=(ga, j), device_id_type=MESH))
+
+    def spread_of(k):
+        return min(k // ny, groups - k // ny) + min(k % ny, ny - k % ny)
+
+    near = sorted(range(1, planes), key=spread_of)
+    around = [(lax.rem(ga + k // ny, groups), lax.rem(y + k % ny, ny), k // ny) for k in near]
     extra = 0
     for aa, yy, off in around:
         if off:
             pl.semaphore_signal(barrier, inc=1, device_id=(aa, at(z, yy, core)), device_id_type=MESH)
             extra += 1
-    lax.fori_loop(1, parts, greet, 0)
-
     for b in range(2):
         row = civ_ref[pl.ds(lax.rem(batch_ref[2 * ga + b], rows_dev), 1), :]
         for t in range(cuts):
@@ -141,11 +154,7 @@
             rows_s, table.at[slot], ts.at[j], tr.at[slot], device_id=(ga, j), device_id_type=MESH
         )
 
-    def send_row(d, c):
-        row_copy(lax.rem(me + d, parts), me).start()
-        return c
-
-    lax.fori_loop(1, parts, send_row, 0)
+    each(lambda j: row_copy(j, me).start())
 
     right, left = lax.rem(ga + 1, groups), lax.rem(ga + groups - 1, groups)
     half_rows = rows_dev // 2
@@ -242,8 +251,10 @@
     halves = split(jnp.concatenate([t_ref[0], t_ref[1]], axis=0))
     full = jnp.concatenate(halves, axis=1)
 
-    def mux(got, high):
-        for bit in range(3):
+    levels = 3 if total_rows % 64 == 0 else 0
+
+    def mux(got, high, low_bit, count):
+        for bit in range(low_bit, low_bit + count):
             n = got.shape[0] // 2
             got = got.reshape(n, 2, 8, LANES)
             mask = jnp.broadcast_to(jnp.bitwise_and(high, 1 << bit)[None], (n, 8, LANES)) != 0
@@ -251,9 +262,10 @@
         return got
 
     sub = lax.broadcasted_iota(I32, (8, LANES), 0)
-    tall = lax.broadcasted_iota(I32, (LANES, LANES), 0)
-
-    def look_up(i, c):
+    tall = lax.broadcasted_iota(I32, (LANES, LANES), 0).astype(F32).astype(BF16)
+    blank_hot, full_hot = jnp.zeros((LANES, LANES), BF16), jnp.ones((LANES, LANES), BF16)
+
+    def look_up(i):
         start = pl.multiple_of(8 * i, 8)
         for lt in range(cuts):
             src = look_ref[lt, pl.ds(start, 8), :]
@@ -266,40 +278,50 @@
                 for base in range(0, total_rows, chunk):
                     for b in range(2):
                         got = texp[b, base : base + chunk].reshape(chunk * 8, LANES)
-                        got = mux(lanes_of(got, index).reshape(chunk, 8, LANES), high)
+                        got = mux(lanes_of(got, index).reshape(chunk, 8, LANES), high, 0, 3)
                         for k in range(chunk // 8):
                             acc[b] = jnp.where(group == base // 8 + k, got[k], acc[b])
             else:
                 for r in range(0, 8, 2):
-                    hot = jnp.concatenate(
-                        [(tall == low[r + k : r + k + 1]).astype(F32).astype(BF16) for k in range(2)], axis=1
-                    )
+                    hot = []
+                    for k in range(2):
+                        line = jnp.broadcast_to(low[r + k : r + k + 1], (16, LANES)).astype(F32).astype(BF16)
+                        hot.append(jnp.where(tall == jnp.concatenate([line] * 8, axis=0), full_hot, blank_hot))
+                    hot = jnp.concatenate(hot, axis=1)
                     found = dot(full, jnp.concatenate([hot, hot], axis=0), NN)
                     for k in range(2):
                         wide = jnp.broadcast_to(high[r + k : r + k + 1], (8, LANES))
                         near = jnp.bitwise_and(wide, 7) == sub
-                        group = lax.shift_right_logical(wide, 3)
+                        block = lax.shift_right_logical(wide, 3 + levels)
                         for b in range(2):
                             mine = found[b * total_rows : (b + 1) * total_rows, k * LANES : (k + 1) * LANES]
-                            mine = mine.reshape(total_rows // 8, 8, LANES)
+                            mine = mux(mine.reshape(total_rows // 8, 8, LANES), wide, 3, levels)
                             best = mine[0]
-                            for q in range(1, total_rows // 8):
-                                best = jnp.where(group == q, mine[q], best)
+                            for q in range(1, mine.shape[0]):
+                                best = jnp.where(block == q, mine[q], best)
                             value = jnp.sum(jnp.where(near, best, 0.0), axis=0, keepdims=True)
                             acc[b] = jnp.where(sub == r + k, value, acc[b])
             factor = sign_ref[lt, pl.ds(start, 8), :]
             vals_ref[0, lt, pl.ds(start, 8), :] = acc[0] * factor
             vals_ref[1, lt, pl.ds(start, 8), :] = acc[1] * factor
+
+    def look_two(i, c):
+        look_up(2 * i)
+        look_up(2 * i + 1)
         return c
 
     tiles = slots_deep // 8
-    relay = tiles // 2
-    lax.fori_loop(0, relay, look_up, 0)
+    relay = tiles // 4
+    lax.fori_loop(0, relay, look_two, 0)
     for hop in hops[:2]:
         hop.wait_recv()
     for hop in hops[2:]:
         hop.start()
-    lax.fori_loop(relay, tiles, look_up, 0)
+    lax.fori_loop(relay, tiles // 2, look_two, 0)
+    for i in range(tiles // 2 * 2, tiles):
+        look_up(i)
+    for hop in hops[2:]:
+        hop.wait_recv()
 
     blank = jnp.zeros((LANES - slots_deep, LANES), F32)
     d2 = []
@@ -311,21 +333,12 @@
             [lanes_of(by_slot, inv_ref[:, base : base + LANES]) for base in range(0, deep, LANES)], axis=1
         )))
 
-    for hop in hops[2:]:
-        hop.wait_recv()
     owners = [lax.rem(ga + groups - 1, groups), lax.rem(ga + 1, groups), lax.rem(ga + 2, groups)]
     for k in range(groups - 1):
         more = choose(blk_ref[k], owners[k])
         a_high, a_low = a_high + more[0], a_low + more[1]
     a2 = (a_high.astype(BF16), a_low.astype(BF16))
     a = a_high + a_low
-
-    for b in range(2):
-        from_a = jnp.sum(a * meta[:, 2 + b : 3 + b], axis=0, keepdims=True)
-        for lt in range(cuts):
-            cut = slice(lt * LANES, (lt + 1) * LANES)
-            from_b = jnp.sum(vals_ref[b, lt] * hx_ref[lt], axis=0, keepdims=True)
-            sigma_ref[b : b + 1, cut] = from_a[:, cut] + from_b
 
     def times(left, right, dims):
         n = left[0].shape[0]
@@ -355,81 +368,91 @@
         for lt in range(3):
             k = rg * 3 + lt
             piece = last if lt == 2 else m[:, lt * LANES : (lt + 1) * LANES]
-            tiles_ref[k // per, k % per] = piece[8 * rg : 8 * rg + 8]
-    tiles_ref[parts - 1, per - 1] = jnp.zeros((8, LANES), F32)
-
-    def part_copy(j, slot):
-        return pltpu.make_async_remote_copy(
-            tiles_ref.at[j], got_ref.at[slot], ssem.at[j], rsem.at[slot], device_id=(ga, j), device_id_type=MESH
-        )
-
-    def send(d, c):
-        part_copy(lax.rem(me + d, parts), me).start()
+            tiles_ref[(k // per) % nc, k // per // nc, k % per] = piece[8 * rg : 8 * rg + 8]
+    tiles_ref[nc - 1, parts // nc - 1, per - 1] = jnp.zeros((8, LANES), F32)
+
+    def settled(count, sem):
+        return pltpu.make_async_remote_copy(
+            dummy.at[pl.ds(0, count)], dummy.at[pl.ds(0, count)], sem, sem, device_id=(right, me), device_id_type=MESH
+        )
+
+    chips = parts // nc
+    chip = z * ny + y
+    pair = pltpu.make_async_remote_copy(
+        tiles_ref.at[1 - core], pair_buf, ps, pr, device_id=(ga, at(z, y, 1 - core)), device_id_type=MESH
+    )
+    pair.start()
+
+    def drain_row(k, c):
+        row_copy(far_first(k), me).wait_send()
         return c
 
-    lax.fori_loop(1, parts, send, 0)
-    got_ref[me] = tiles_ref[me]
-
-    def finish(d, c):
-        j = lax.rem(me + d, parts)
-        part_copy(j, j).wait_recv()
+    for b in range(2):
+        from_a = jnp.sum(a * meta[:, 2 + b : 3 + b], axis=0, keepdims=True)
+        for lt in range(cuts):
+            cut = slice(lt * LANES, (lt + 1) * LANES)
+            from_b = jnp.sum(vals_ref[b, lt] * hx_ref[lt], axis=0, keepdims=True)
+            sigma_ref[b : b + 1, cut] = from_a[:, cut] + from_b
+    pair.wait_recv()
+    sums[...] = tiles_ref[core] + pair_buf[...]
+
+    def part_copy(q):
+        return pltpu.make_async_remote_copy(
+            sums.at[q], got_ref.at[chip], ssem, rsem, device_id=(ga, q * nc + core), device_id_type=MESH
+        )
+
+    def send_part(k, c):
+        part_copy(lax.rem(chip + 1 + lax.rem(k + (chips * 5) // 16, chips - 1), chips)).start()
         return c
 
-    lax.fori_loop(1, parts, finish, 0)
+    lax.fori_loop(0, chips - 1, send_part, 0)
+    got_ref[chip] = sums[chip]
+    lax.fori_loop(0, others, drain_row, 0)
+    for hop in hops:
+        hop.wait_send()
+    pair.wait_send()
+    settled((chips - 1) * per, rsem).wait_recv()
     zbuf[z] = jnp.sum(got_ref[...], axis=0)
 
-    def z_copy(zz, slot):
-        return pltpu.make_async_remote_copy(
-            zbuf.at[slot], zbuf.at[slot], zs.at[zz], zr.at[slot], device_id=(ga, at(zz, y, core)), device_id_type=MESH
-        )
-
-    for k in range(1, nz):
-        z_copy(lax.rem(z + k, nz), z).start()
-    for k in range(1, nz):
-        zz = lax.rem(z + k, nz)
-        z_copy(zz, zz).wait_recv()
+    def z_copy(zz):
+        return pltpu.make_async_remote_copy(
+            zbuf.at[z], zbuf.at[z], zs, zr, device_id=(ga, at(zz, y, core)), device_id_type=MESH
+        )
+
+    for k in sorted(range(1, nz), key=lambda k: -min(k, nz - k)):
+        z_copy(lax.rem(z + k, nz)).start()
+    settled((chips - 1) * per, ssem).wait_send()
+    if nz > 1:
+        settled((nz - 1) * per, zr).wait_recv()
 
     def plane_copy(src, aa, yy, slot_a, slot_y):
         return pltpu.make_async_remote_copy(
-            src, gat.at[slot_a, slot_y, core], fs.at[aa, yy], fr.at[slot_a, slot_y],
+            src, gat.at[slot_a, slot_y, core], fs, fr.at[slot_a, slot_y],
             device_id=(aa, at(z, yy, core)), device_id_type=MESH,
         )
 
-    def twin_copy(src, slot_a, slot_y, slot_c):
-        return pltpu.make_async_remote_copy(
-            src, gat.at[slot_a, slot_y, slot_c], cs.at[slot_a, slot_y], cr.at[slot_a, slot_y],
+    def twin_copy(src, slot_a, slot_y):
+        return pltpu.make_async_remote_copy(
+            src, gat.at[slot_a, slot_y, core], cs, cr,
             device_id=(ga, at(z, y, 1 - core)), device_id_type=MESH,
         )
 
-    for aa, yy, _ in around:
+    for aa, yy, _ in around[::-1]:
         plane_copy(zbuf, aa, yy, ga, y).start()
-    twin_copy(zbuf, ga, y, core).start()
+    twin_copy(zbuf, ga, y).start()
     gat[ga, y, core] = zbuf[...]
     for aa, yy, _ in around:
         plane_copy(zbuf, aa, yy, aa, yy).wait_recv()
-        twin_copy(gat.at[aa, yy, core], aa, yy, core).start()
-    for aa, yy, _ in [(ga, y, 0)] + around:
-        twin_copy(zbuf, aa, yy, 1 - core).wait_recv()
-
-    def drain(d, c):
-        j = lax.rem(me + d, parts)
-        part_copy(j, j).wait_send()
-        row_copy(j, j).wait_send()
-        return c
-
-    lax.fori_loop(1, parts, drain, 0)
-    for hop in hops:
-        hop.wait_send()
-    for k in range(1, nz):
-        z_copy(lax.rem(z + k, nz), z).wait_send()
-    for aa, yy, _ in around:
-        plane_copy(zbuf, aa, yy, ga, y).wait_send()
-    for aa, yy, _ in [(ga, y, 0)] + around:
-        twin_copy(zbuf, aa, yy, core).wait_send()
+        twin_copy(gat.at[aa, yy, core], aa, yy).start()
+    if nz > 1:
+        settled((nz - 1) * per, zs).wait_send()
+    settled((planes - 1) * nz * per, fs).wait_send()
+    settled(planes * nz * per, cr).wait_recv()
+    settled(planes * nz * per, cs).wait_send()
 
 
 def place_kernel(groups, shape, slots, pairs, norm, exc_ref, gat, sigma_in, sigma_ref, density_ref, same_ref, mixed_ref,
-                 r_ref, wide_ref):
+                 r_ref, t_ref, wide_ref):
     nz, ny, nc = shape
     per = 64 // (nz * ny * nc)
     string = slots + 1
@@ -443,32 +466,42 @@
     weights = jnp.where((lane == SHIFT) | (lane == SHIFT + HALF - 1), 0.5, 1.0)
     weights = jnp.where((lane >= SHIFT) & (lane < SHIFT + HALF), weights, 0.0)
     strip = lax.broadcasted_iota(I32, (1, LANES), 1)
-    mixed = jnp.zeros((deep, deep), F32)
-    upper = jnp.zeros((deep, deep), F32)
+    wide = lax.broadcasted_iota(I32, (1, 2 * LANES), 1)
+    span = -(-groups * ROWS // LANES) * LANES
+    p_all = jnp.zeros((1, span), F32)
+    exts = []
     for g in range(groups):
+        rows = slice(g * ROWS, (g + 1) * ROWS)
         for rg in range(ROWS // 8):
             for lt in range(3):
                 k = rg * 3 + lt
                 j, s = k // per, k % per
-                r_ref[8 * rg : 8 * rg + 8, lt * LANES : (lt + 1) * LANES] = gat[
+                r_ref[g * ROWS + 8 * rg : g * ROWS + 8 * rg + 8, lt * LANES : (lt + 1) * LANES] = gat[
                     g, (j // nc) % ny, j % nc, j // (ny * nc), s
                 ]
         ids = exc_ref[1, 2 * g : 2 * g + 2, :].astype(F32)
-        p_row = packed_row(wide_ref, ids[0:1], ids[1:2], slots, float(pairs), float(pairs))
-        placing = (lax.broadcasted_iota(I32, (deep, ROWS), 0).astype(F32) == p_row[:, 0:ROWS]).astype(BF16)
-        mixed = mixed + dot2(placing, split(r_ref[...]), NN)
-        half = barrel(r_ref[:, 2 * LANES :] * weights, amount, 7)
-        both = jnp.concatenate([jnp.where(first, half, 0.0), jnp.where(first, 0.0, half)], axis=1)
+        p_row = packed_row(wide_ref.at[g], ids[0:1], ids[1:2], slots, float(pairs), float(pairs))
+        p_row = jnp.where(wide < ROWS, p_row, 0.0)
+        p_row = jnp.concatenate([p_row, jnp.zeros((1, span - 2 * LANES), F32)], axis=1)
+        p_all = p_all + (pltpu.roll(p_row, g * ROWS, 1) if g else p_row)
         ends = []
         for b in range(2):
-            line = wide_ref[b : b + 1, :]
+            line = wide_ref[g, b : b + 1, :]
             again = pltpu.roll(line, string, 1)
             line = jnp.where(strip < slots, line, jnp.where(strip == slots, float(pairs), again))
             ends.append(line)
-        ext = jnp.concatenate(ends, axis=1)
-        right = (lax.broadcasted_iota(I32, (deep, 2 * LANES), 0).astype(F32) == ext).astype(BF16)
-        t = sum(dot(p, right, NT) for p in split(both))
-        upper = upper + dot2(placing, split(t), NN)
+        exts.append(jnp.concatenate(ends, axis=1))
+    exts = jnp.concatenate(exts + [jnp.zeros((8 - groups, 2 * LANES), F32)], axis=0).T
+    for g in range(groups):
+        rows = slice(g * ROWS, (g + 1) * ROWS)
+        half = barrel(r_ref[rows, 2 * LANES :] * weights, amount, 7)
+        both = split(jnp.concatenate([jnp.where(first, half, 0.0), jnp.where(first, 0.0, half)], axis=1))
+        right = (lax.broadcasted_iota(I32, (2 * LANES, deep), 1).astype(F32) == exts[:, g : g + 1]).astype(BF16)
+        twice = dot(jnp.concatenate(both, axis=0), right, NN)
+        t_ref[rows, :] = twice[:ROWS] + twice[ROWS:]
+    placing = (lax.broadcasted_iota(I32, (deep, groups * ROWS), 0).astype(F32) == p_all[:, : groups * ROWS]).astype(BF16)
+    mixed = dot2(placing, split(r_ref[...]), NN)
+    upper = dot2(placing, split(t_ref[...]), NN)
     root = math.sqrt(norm)
     same = upper + upper.T
     density_ref[0:1, :] = same[pairs : pairs + 1, 0:pairs] * (1.0 / root)
@@ -515,15 +548,17 @@
             pltpu.VMEM((max(groups - 1, 2), rows_dev, width), F32),
             pltpu.VMEM((8, deep), F32),
             pltpu.VMEM((8, LANES), F32),
-            pltpu.VMEM((parts, per, 8, LANES), F32),
-            pltpu.VMEM((parts, per, 8, LANES), F32),
+            pltpu.VMEM((nc, parts // nc, per, 8, LANES), F32),
+            pltpu.VMEM((parts // nc, per, 8, LANES), F32),
+            pltpu.VMEM((parts // nc, per, 8, LANES), F32),
+            pltpu.VMEM((parts // nc, per, 8, LANES), F32),
             pltpu.VMEM((nz, per, 8, LANES), F32),
+            pltpu.VMEM((groups * ny * nz * per, 8, LANES), F32),
             dma((parts,)), dma((parts,)),
             dma((4,)), dma((4,)),
-            dma((parts,)), dma((parts,)),
-            dma((nz,)), dma((nz,)),
-            dma((groups, ny)), dma((groups, ny)),
-            dma((groups, ny)), dma((groups, ny)),
+            dma, dma, dma, dma, dma, dma, dma,
+            dma((groups, ny)),
+            dma, dma,
         ],
         compiler_params=pltpu.CompilerParams(collective_id=0, has_side_effects=True),
         name="main",
@@ -538,7 +573,7 @@
         ),
         in_specs=[vmem, vmem, vmem],
         out_specs=(vmem, vmem, vmem, vmem),
-        scratch_shapes=[pltpu.VMEM((ROWS, deep), F32), pltpu.VMEM((8, LANES), F32)],
+        scratch_shapes=[pltpu.VMEM((groups * ROWS, deep), F32)] * 2 + [pltpu.VMEM((groups, 8, LANES), F32)],
         name="place",
     )(exc_alpha, gat, sigma))
 

time: 68.6 us -> 62.4 us (0.910)
  Pallas kernels: 67.8 us -> 61.7 us
    pallas_call x1, Pallas kernels: 62.5 us -> 56.7 us  [body(): pl.pallas_call(functools.partial(main_kernel, groups, shape, slots, pairs...]
where the time goes in v4:
time: 62.4 us; the launch traced here: 62.3 us
  Pallas kernels  61.7 us (99%)
  between operations  0.64 us (1%)
    pallas_call x1, Pallas kernels, body(): pl.pallas_call(functools.partial(main_kernel, groups, shape, slots, pairs...  56.7 us
    pallas_call x1, Pallas kernels, body(): pl.pallas_call(functools.partial(place_kernel, groups, shape, slots, pair...  4.93 us

profile of v4, /device:TPU:1, one launch (start us, length us, event | category | flops | bytes accessed | tf_op | source)
XLA Modules:
  0.0 62.3 jit_solution(5439625801472638022)
XLA Ops:
  0.6 56.7 %main.1 = (f32[2,384]{1,0:T(2,128)}, f32[4,4,2,8,1,8,128]{6,5,4,3,2,1,0:T(8,128)}) custom-call(s32[8]{0:T(128)} %batch_ref.1, s32[3,8,81]{2,1,0:T(8,128)} %exc_ref.3, s32[3,81,384]{2,1,0:T(8,128)} %bitcast.1, f32[324]{0:T(512)} %h_ref.1, f32[256,384]{1,0:T(8,128)} %civ_ref.1), custom_call_target="tpu_custom_call" | custom-call | tf_op jit(solution)/shard_map/main/pallas_call | solution.py:529
  57.4 4.9 %place.1 = (f32[2,384]{1,0:T(2,128)}, f32[2,324]{1,0:T(2,128)}, f32[324,324]{1,0:T(8,128)}, f32[324,324]{1,0:T(8,128)}) custom-call(s32[3,8,81]{2,1,0:T(8,128)} %exc_ref.3, f32[4,4,2,8,1,8,128]{6,5,4,3,2,1,0:T(8,128)} %get-tuple-element.6.gat, f32[2,384]{1,0:T(2,128)} %get-tuple-element.7.sigma_in), custom_call_target="tpu_custom_call" | custom-call | tf_op jit(solution)/shard_map/place/pallas_call | solution.py:566

commit v5 on v4

--- a/solution.py
+++ b/solution.py
@@ -64,10 +64,10 @@
     return jnp.where(lane < 2 * string, out, float(EMPTY))
 
 
-def main_kernel(groups, shape, slots, pairs, batch_ref, exc_ref, beta_ref, h_ref, civ_ref, sigma_ref, gat,
-                pair_ref, look_ref, sign_ref, hx_ref, inv_ref, rows_s, table, texp, t_ref, vals_ref, blk_ref, line_ref,
+def main_kernel(groups, shape, slots, pairs, batch_ref, exc_ref, beta_hbm, h_ref, civ_hbm, sigma_ref, gat,
+                beta_ref, civ_ref, pair_ref, look_ref, sign_ref, hx_ref, inv_ref, rows_s, table, texp, t_ref, vals_ref, blk_ref, line_ref,
                 wide_ref, tiles_ref, pair_buf, sums, got_ref, zbuf, dummy,
-                ts, tr, xs, xr, ps, pr, ssem, rsem, zs, zr, fs, fr, cs, cr):
+                in_sem, ts, tr, xs, xr, ps, pr, ssem, rsem, zs, zr, fs, fr, cs, cr):
     nz, ny, nc = shape
     parts = nz * ny * nc
     per = 64 // parts
@@ -85,6 +85,9 @@
     def at(zz, yy, cc):
         return (zz * ny + yy) * nc + cc
 
+    loads = [pltpu.make_async_copy(civ_hbm, civ_ref, in_sem.at[0]), pltpu.make_async_copy(beta_hbm, beta_ref, in_sem.at[1])]
+    for load in loads:
+        load.start()
     barrier = pltpu.get_barrier_semaphore()
     others = parts - 1
     burst = 7 if others % 7 == 0 else 1
@@ -102,16 +105,12 @@
 
     each(lambda j: pl.semaphore_signal(barrier, inc=1, device_id=(ga, j), device_id_type=MESH))
 
-    def spread_of(k):
-        return min(k // ny, groups - k // ny) + min(k % ny, ny - k % ny)
-
-    near = sorted(range(1, planes), key=spread_of)
-    around = [(lax.rem(ga + k // ny, groups), lax.rem(y + k % ny, ny), k // ny) for k in near]
-    extra = 0
-    for aa, yy, off in around:
-        if off:
-            pl.semaphore_signal(barrier, inc=1, device_id=(aa, at(z, yy, core)), device_id_type=MESH)
-            extra += 1
+    for d in range(1, groups):
+        pl.semaphore_signal(barrier, inc=1, device_id=(lax.rem(ga + d, groups), me), device_id_type=MESH)
+    extra = groups - 1
+
+    for load in loads:
+        load.wait()
     for b in range(2):
         row = civ_ref[pl.ds(lax.rem(batch_ref[2 * ga + b], rows_dev), 1), :]
         for t in range(cuts):
@@ -265,49 +264,62 @@
     tall = lax.broadcasted_iota(I32, (LANES, LANES), 0).astype(F32).astype(BF16)
     blank_hot, full_hot = jnp.zeros((LANES, LANES), BF16), jnp.ones((LANES, LANES), BF16)
 
-    def look_up(i):
+    def match(lines):
+        hot = []
+        for low, _ in lines:
+            line = jnp.broadcast_to(low, (16, LANES)).astype(F32).astype(BF16)
+            hot.append(jnp.where(tall == jnp.concatenate([line] * 8, axis=0), full_hot, blank_hot))
+        hot = jnp.concatenate(hot, axis=1) if len(hot) > 1 else hot[0]
+        found = dot(full, jnp.concatenate([hot, hot], axis=0), NN)
+        values = []
+        for k, (_, high) in enumerate(lines):
+            wide = jnp.broadcast_to(high, (8, LANES))
+            near = jnp.bitwise_and(wide, 7) == sub
+            block = lax.shift_right_logical(wide, 3 + levels)
+            both = []
+            for b in range(2):
+                mine = found[b * total_rows : (b + 1) * total_rows, k * LANES : (k + 1) * LANES]
+                mine = mux(mine.reshape(total_rows // 8, 8, LANES), wide, 3, levels)
+                best = mine[0]
+                for q in range(1, mine.shape[0]):
+                    best = jnp.where(block == q, mine[q], best)
+                both.append(jnp.sum(jnp.where(near, best, 0.0), axis=0, keepdims=True))
+            values.append(both)
+        return values
+
+    def look_up(i, live):
         start = pl.multiple_of(8 * i, 8)
+        low, high, acc = [], [], []
         for lt in range(cuts):
             src = look_ref[lt, pl.ds(start, 8), :]
-            low = jnp.bitwise_and(src, 127)
-            high = lax.shift_right_logical(src, 7)
-            acc = [jnp.zeros((8, LANES), F32)] * 2
-            if lt == 0:
-                group = lax.shift_right_logical(high, 3)
-                index = jnp.broadcast_to(low[None], (chunk, 8, LANES)).reshape(chunk * 8, LANES)
-                for base in range(0, total_rows, chunk):
-                    for b in range(2):
-                        got = texp[b, base : base + chunk].reshape(chunk * 8, LANES)
-                        got = mux(lanes_of(got, index).reshape(chunk, 8, LANES), high, 0, 3)
-                        for k in range(chunk // 8):
-                            acc[b] = jnp.where(group == base // 8 + k, got[k], acc[b])
-            else:
-                for r in range(0, 8, 2):
-                    hot = []
-                    for k in range(2):
-                        line = jnp.broadcast_to(low[r + k : r + k + 1], (16, LANES)).astype(F32).astype(BF16)
-                        hot.append(jnp.where(tall == jnp.concatenate([line] * 8, axis=0), full_hot, blank_hot))
-                    hot = jnp.concatenate(hot, axis=1)
-                    found = dot(full, jnp.concatenate([hot, hot], axis=0), NN)
-                    for k in range(2):
-                        wide = jnp.broadcast_to(high[r + k : r + k + 1], (8, LANES))
-                        near = jnp.bitwise_and(wide, 7) == sub
-                        block = lax.shift_right_logical(wide, 3 + levels)
-                        for b in range(2):
-                            mine = found[b * total_rows : (b + 1) * total_rows, k * LANES : (k + 1) * LANES]
-                            mine = mux(mine.reshape(total_rows // 8, 8, LANES), wide, 3, levels)
-                            best = mine[0]
-                            for q in range(1, mine.shape[0]):
-                                best = jnp.where(block == q, mine[q], best)
-                            value = jnp.sum(jnp.where(near, best, 0.0), axis=0, keepdims=True)
-                            acc[b] = jnp.where(sub == r + k, value, acc[b])
+            low.append(jnp.bitwise_and(src, 127))
+            high.append(lax.shift_right_logical(src, 7))
+            acc.append([jnp.zeros((8, LANES), F32)] * 2)
+        direct = 1 if live == 8 else 0
+        if direct:
+            group = lax.shift_right_logical(high[0], 3)
+            index = jnp.broadcast_to(low[0][None], (chunk, 8, LANES)).reshape(chunk * 8, LANES)
+            for base in range(0, total_rows, chunk):
+                for b in range(2):
+                    got = texp[b, base : base + chunk].reshape(chunk * 8, LANES)
+                    got = mux(lanes_of(got, index).reshape(chunk, 8, LANES), high[0], 0, 3)
+                    for k in range(chunk // 8):
+                        acc[0][b] = jnp.where(group == base // 8 + k, got[k], acc[0][b])
+        spots = [(lt, r) for lt in range(direct, cuts) for r in range(live)]
+        for n in range(0, len(spots), 2):
+            some = spots[n : n + 2]
+            values = match([(low[lt][r : r + 1], high[lt][r : r + 1]) for lt, r in some])
+            for (lt, r), both in zip(some, values):
+                for b in range(2):
+                    acc[lt][b] = jnp.where(sub == r, both[b], acc[lt][b])
+        for lt in range(cuts):
             factor = sign_ref[lt, pl.ds(start, 8), :]
-            vals_ref[0, lt, pl.ds(start, 8), :] = acc[0] * factor
-            vals_ref[1, lt, pl.ds(start, 8), :] = acc[1] * factor
+            for b in range(2):
+                vals_ref[b, lt, pl.ds(start, 8), :] = acc[lt][b] * factor
 
     def look_two(i, c):
-        look_up(2 * i)
-        look_up(2 * i + 1)
+        look_up(2 * i, 8)
+        look_up(2 * i + 1, 8)
         return c
 
     tiles = slots_deep // 8
@@ -319,7 +331,7 @@
         hop.start()
     lax.fori_loop(relay, tiles // 2, look_two, 0)
     for i in range(tiles // 2 * 2, tiles):
-        look_up(i)
+        look_up(i, min(8, slots - 8 * i))
     for hop in hops[2:]:
         hop.wait_recv()
 
@@ -425,28 +437,89 @@
     if nz > 1:
         settled((nz - 1) * per, zr).wait_recv()
 
-    def plane_copy(src, aa, yy, slot_a, slot_y):
+    ring = groups
+    fx, fy = 1 - core, core
+
+    def along(first, second):
+        return (
+            lax.rem(ga + first * fx + second * fy + 2 * ring, ring),
+            lax.rem(y + first * fy + second * fx + 2 * ring, ring),
+        )
+
+    def piece(first, second, part):
+        aa, yy = along(first, second)
+        if part is None:
+            return gat.at[aa, yy, core]
+        return gat.at[aa, yy, core, pl.ds(part * (nz // 2), nz // 2)]
+
+    def push(src, first, second, to_first, to_second, sem, part=None):
+        aa, yy = along(to_first, to_second)
         return pltpu.make_async_remote_copy(
-            src, gat.at[slot_a, slot_y, core], fs, fr.at[slot_a, slot_y],
-            device_id=(aa, at(z, yy, core)), device_id_type=MESH,
-        )
-
-    def twin_copy(src, slot_a, slot_y):
+            src, piece(first, second, part), fs, fr.at[sem], device_id=(aa, at(z, yy, core)), device_id_type=MESH
+        )
+
+    def twin_copy(src, first, second):
         return pltpu.make_async_remote_copy(
-            src, gat.at[slot_a, slot_y, core], cs, cr,
-            device_id=(ga, at(z, y, 1 - core)), device_id_type=MESH,
-        )
-
-    for aa, yy, _ in around[::-1]:
-        plane_copy(zbuf, aa, yy, ga, y).start()
-    twin_copy(zbuf, ga, y).start()
+            src, piece(first, second, None), cs, cr, device_id=(ga, at(z, y, 1 - core)), device_id_type=MESH
+        )
+
+    steps = [1] if ring == 2 else [-1, 1, 2]
+    sides = [1] if ring == 2 else [-1, 1]
+    row_of = [0] + steps
+
+    def sem_of(f, kind):
+        return f * 4 + kind
+
+    def own_block(f):
+        return zbuf if f == 0 else piece(row_of[f], 0, None)
+
+    def send_second(f):
+        for n, side in enumerate(sides):
+            push(own_block(f), row_of[f], 0, 0, side, sem_of(f, n)).start()
+
+    def await_first(n):
+        push(zbuf, steps[n], 0, 0, 1, 16 + n).wait_recv()
+        twin_copy(piece(steps[n], 0, None), steps[n], 0).start()
+        send_second(n + 1)
+
+    def await_second(f):
+        for n, side in enumerate(sides):
+            push(zbuf, row_of[f], -side, 0, side, sem_of(f, n)).wait_recv()
+            if ring == 4:
+                push(piece(row_of[f], -side, n), row_of[f], -side, 0, side, sem_of(f, 2 + n), n).start()
+            twin_copy(piece(row_of[f], -side, None), row_of[f], -side).start()
+
+    def await_halves(f):
+        if ring == 4:
+            for n in range(2):
+                push(piece(row_of[f], 2, n), row_of[f], 2, 0, 1, sem_of(f, 2 + n), n).wait_recv()
+            twin_copy(piece(row_of[f], 2, None), row_of[f], 2).start()
+
+    for n in range(len(steps) - 1, -1, -1):
+        back = steps[n] if ring == 2 else (steps[n] if steps[n] == 2 else -steps[n])
+        push(zbuf, 0, 0, back, 0, 16 + n).start()
+    send_second(0)
+    twin_copy(zbuf, 0, 0).start()
     gat[ga, y, core] = zbuf[...]
-    for aa, yy, _ in around:
-        plane_copy(zbuf, aa, yy, aa, yy).wait_recv()
-        twin_copy(gat.at[aa, yy, core], aa, yy).start()
+    if ring == 2:
+        await_first(0)
+        await_second(0)
+        await_second(1)
+    else:
+        await_first(0)
+        await_first(1)
+        await_second(0)
+        await_first(2)
+        await_second(1)
+        await_second(2)
+        await_halves(0)
+        await_second(3)
+        for f in (1, 2, 3):
+            await_halves(f)
+    sent = len(steps) * nz * per + len(row_of) * len(sides) * nz * per + (8 * (nz // 2) * per if ring == 4 else 0)
     if nz > 1:
         settled((nz - 1) * per, zs).wait_send()
-    settled((planes - 1) * nz * per, fs).wait_send()
+    settled(sent, fs).wait_send()
     settled(planes * nz * per, cr).wait_recv()
     settled(planes * nz * per, cs).wait_send()
 
@@ -499,9 +572,11 @@
         right = (lax.broadcasted_iota(I32, (2 * LANES, deep), 1).astype(F32) == exts[:, g : g + 1]).astype(BF16)
         twice = dot(jnp.concatenate(both, axis=0), right, NN)
         t_ref[rows, :] = twice[:ROWS] + twice[ROWS:]
-    placing = (lax.broadcasted_iota(I32, (deep, groups * ROWS), 0).astype(F32) == p_all[:, : groups * ROWS]).astype(BF16)
-    mixed = dot2(placing, split(r_ref[...]), NN)
-    upper = dot2(placing, split(t_ref[...]), NN)
+    tall = -(-(pairs + 1) // 8) * 8
+    placing = (lax.broadcasted_iota(I32, (tall, groups * ROWS), 0).astype(F32) == p_all[:, : groups * ROWS]).astype(BF16)
+    placed = dot2(placing, split(jnp.concatenate([r_ref[...], t_ref[...]], axis=1)), NN)
+    mixed = placed[:, :deep]
+    upper = jnp.concatenate([placed[:, deep:], jnp.zeros((deep - tall, deep), F32)], axis=0)
     root = math.sqrt(norm)
     same = upper + upper.T
     density_ref[0:1, :] = same[pairs : pairs + 1, 0:pairs] * (1.0 / root)
@@ -513,6 +588,7 @@
 def body(shape, civec, batch_index, exc_alpha, exc_beta, one_body):
     vmem = pl.BlockSpec(memory_space=pltpu.VMEM)
     smem = pl.BlockSpec(memory_space=pltpu.SMEM)
+    anywhere = pl.BlockSpec(memory_space=pl.ANY)
     nz, ny, nc = shape
     parts = nz * ny * nc
     per = 64 // parts
@@ -532,9 +608,11 @@
             jax.ShapeDtypeStruct((batch, width), F32),
             jax.ShapeDtypeStruct((groups, ny, nc, nz, per, 8, LANES), F32),
         ),
-        in_specs=[smem, vmem, vmem, vmem, vmem],
+        in_specs=[smem, vmem, anywhere, vmem, anywhere],
         out_specs=(vmem, vmem),
         scratch_shapes=[
+            pltpu.VMEM((3, slots, width), I32),
+            pltpu.VMEM((rows_dev, width), F32),
             pltpu.VMEM((cuts, slots_deep, LANES), I32),
             pltpu.VMEM((cuts, slots_deep, LANES), I32),
             pltpu.VMEM((cuts, slots_deep, LANES), F32),
@@ -554,10 +632,11 @@
             pltpu.VMEM((parts // nc, per, 8, LANES), F32),
             pltpu.VMEM((nz, per, 8, LANES), F32),
             pltpu.VMEM((groups * ny * nz * per, 8, LANES), F32),
+            dma((2,)),
             dma((parts,)), dma((parts,)),
             dma((4,)), dma((4,)),
             dma, dma, dma, dma, dma, dma, dma,
-            dma((groups, ny)),
+            dma((20,)),
             dma, dma,
         ],
         compiler_params=pltpu.CompilerParams(collective_id=0, has_side_effects=True),

time: 62.4 us -> 65.4 us (1.048)
  Pallas kernels: 61.7 us -> 64.6 us
    pallas_call x1, Pallas kernels: 56.7 us -> 60.1 us  [body(): pl.pallas_call(functools.partial(main_kernel, groups, shape, slots, pairs...]
where the time goes in v5:
time: 65.4 us; the launch traced here: 65.3 us
  Pallas kernels  64.6 us (99%)
    pallas_call x1, Pallas kernels, body(): pl.pallas_call(functools.partial(main_kernel, groups, shape, slots, pairs...  60.1 us
    pallas_call x1, Pallas kernels, body(): pl.pallas_call(functools.partial(place_kernel, groups, shape, slots, pair...  4.55 us

profile of v5, /device:TPU:1, one launch (start us, length us, event | category | flops | bytes accessed | tf_op | source)
XLA Modules:
  0.0 65.3 jit_solution(14700575681732220824)
XLA Ops:
  0.6 60.1 %main.1 = (f32[2,384]{1,0:T(2,128)}, f32[4,4,2,8,1,8,128]{6,5,4,3,2,1,0:T(8,128)}) custom-call(s32[8]{0:T(128)} %batch_ref.1, s32[3,8,81]{2,1,0:T(8,128)} %exc_ref.3, s32[3,81,384]{2,1,0:T(8,128)} %bitcast.1, f32[324]{0:T(512)} %h_ref.1, f32[256,384]{1,0:T(8,128)} %civ_hbm.1), custom_call_target="tpu_custom_call" | custom-call | tf_op jit(solution)/shard_map/main/pallas_call | solution.py:605
  60.7 4.6 %place.1 = (f32[2,384]{1,0:T(2,128)}, f32[2,324]{1,0:T(2,128)}, f32[324,324]{1,0:T(8,128)}, f32[324,324]{1,0:T(8,128)}) custom-call(s32[3,8,81]{2,1,0:T(8,128)} %exc_ref.3, f32[4,4,2,8,1,8,128]{6,5,4,3,2,1,0:T(8,128)} %get-tuple-element.6.gat, f32[2,384]{1,0:T(2,128)} %get-tuple-element.7.sigma_in), custom_call_target="tpu_custom_call" | custom-call | tf_op jit(solution)/shard_map/place/pallas_call | solution.py:645

commit v6 on v5

--- a/solution.py
+++ b/solution.py
@@ -66,8 +66,8 @@
 
 def main_kernel(groups, shape, slots, pairs, batch_ref, exc_ref, beta_hbm, h_ref, civ_hbm, sigma_ref, gat,
                 beta_ref, civ_ref, pair_ref, look_ref, sign_ref, hx_ref, inv_ref, rows_s, table, texp, t_ref, vals_ref, blk_ref, line_ref,
-                wide_ref, tiles_ref, pair_buf, sums, got_ref, zbuf, dummy,
-                in_sem, ts, tr, xs, xr, ps, pr, ssem, rsem, zs, zr, fs, fr, cs, cr):
+                wide_ref, tiles_ref, pair_buf, sums, y_got, y_sum, got_ref, zbuf, dummy,
+                in_sem, ts, tr, ys, yr, ws, wr, vs, vr, xs, xr, ps, pr, ssem, rsem, zs, zr, fs, fr, cs, cr):
     nz, ny, nc = shape
     parts = nz * ny * nc
     per = 64 // parts
@@ -89,26 +89,20 @@
     for load in loads:
         load.start()
     barrier = pltpu.get_barrier_semaphore()
-    others = parts - 1
-    burst = 7 if others % 7 == 0 else 1
-
-    def far_first(k):
-        return lax.rem(me + 1 + lax.rem(k + (others * 5) // 16, others), parts)
-
-    def each(action):
-        def step(k, c):
-            for i in range(burst):
-                action(far_first(burst * k + i))
-            return c
-
-        lax.fori_loop(0, others // burst, step, 0)
-
-    each(lambda j: pl.semaphore_signal(barrier, inc=1, device_id=(ga, j), device_id_type=MESH))
-
-    for d in range(1, groups):
-        pl.semaphore_signal(barrier, inc=1, device_id=(lax.rem(ga + d, groups), me), device_id_type=MESH)
-    extra = groups - 1
-
+    twin = at(z, y, 1 - core)
+    z_far = sorted(range(1, nz), key=lambda k: -min(k, nz - k))
+    y_far = sorted(range(1, ny), key=lambda k: -min(k, ny - k))
+    for k in z_far:
+        pl.semaphore_signal(barrier, inc=1, device_id=(ga, at(lax.rem(z + k, nz), y, core)), device_id_type=MESH)
+
+    def spread_of(k):
+        return min(k // ny, groups - k // ny) + min(k % ny, ny - k % ny)
+
+    near = sorted(range(1, planes), key=spread_of)
+    around = [(lax.rem(ga + k // ny, groups), lax.rem(y + k % ny, ny), k // ny) for k in near]
+    for aa, yy, _ in around[::-1]:
+        pl.semaphore_signal(barrier, inc=1, device_id=(aa, at(z, yy, core)), device_id_type=MESH)
+    pl.semaphore_signal(barrier, inc=1, device_id=(ga, twin), device_id_type=MESH)
     for load in loads:
         load.wait()
     for b in range(2):
@@ -142,18 +136,32 @@
             acc = jnp.concatenate([acc, jnp.full((LANES - size, LANES), LANES - 1, I32)], axis=0)
         inv_ref[lt * LANES : (lt + 1) * LANES, base : base + LANES] = acc.T
 
-    early = len(blocks) // 2
+    early = 2
     for block in blocks[:early]:
         invert(*block)
 
-    pl.semaphore_wait(barrier, parts - 1 + extra)
-
-    def row_copy(j, slot):
-        return pltpu.make_async_remote_copy(
-            rows_s, table.at[slot], ts.at[j], tr.at[slot], device_id=(ga, j), device_id_type=MESH
-        )
-
-    each(lambda j: row_copy(j, me).start())
+    pl.semaphore_wait(barrier, nz - 1 + planes - 1 + 1)
+
+    def row_copy(to_z, slot_z):
+        return pltpu.make_async_remote_copy(
+            rows_s, table.at[y, core, slot_z], ts.at[to_z], tr.at[slot_z],
+            device_id=(ga, at(to_z, y, core)), device_id_type=MESH,
+        )
+
+    def line_copy(to_y, slot_y):
+        return pltpu.make_async_remote_copy(
+            table.at[y, core], table.at[slot_y, core], ys.at[to_y], yr.at[slot_y],
+            device_id=(ga, at(z, to_y, core)), device_id_type=MESH,
+        )
+
+    def twin_line(slot_y, slot_c):
+        return pltpu.make_async_remote_copy(
+            table.at[slot_y, core], table.at[slot_y, slot_c], ws.at[slot_y], wr.at[slot_y],
+            device_id=(ga, twin), device_id_type=MESH,
+        )
+
+    for k in z_far:
+        row_copy(lax.rem(z + k, nz), z).start()
 
     right, left = lax.rem(ga + 1, groups), lax.rem(ga + groups - 1, groups)
     half_rows = rows_dev // 2
@@ -174,7 +182,7 @@
         hops = hops[:1]
     for hop in hops[:2]:
         hop.start()
-    table[me] = rows_s[...]
+    table[y, core, z] = rows_s[...]
 
     for block in blocks[early:]:
         invert(*block)
@@ -229,21 +237,34 @@
 
     a_high, a_low = choose(civ_ref[...], ga)
 
-    def arrive(j):
-        for b in range(2):
-            for t in range(cuts):
-                line = table[j, b * cuts + t : b * cuts + t + 1, :]
-                texp[b, cuts * j + t] = jnp.broadcast_to(line, (8, LANES))
-                t_ref[b, pl.ds(cuts * j + t, 1), :] = line
-
-    def finish_row(d, c):
-        j = lax.rem(me + d, parts)
-        row_copy(j, j).wait_recv()
-        arrive(j)
-        return c
-
-    arrive(me)
-    lax.fori_loop(1, parts, finish_row, 0)
+    def arrive(yy, cc):
+        def step(zz, c):
+            for b in range(2):
+                for t in range(cuts):
+                    line = table[yy, cc, zz, b * cuts + t : b * cuts + t + 1, :]
+                    spot = cuts * at(zz, yy, cc) + t
+                    texp[b, spot] = jnp.broadcast_to(line, (8, LANES))
+                    t_ref[b, pl.ds(spot, 1), :] = line
+            return c
+
+        lax.fori_loop(0, nz, step, 0)
+
+    for k in z_far[::-1]:
+        zz = lax.rem(z + k, nz)
+        row_copy(zz, zz).wait_recv()
+    for k in y_far:
+        line_copy(lax.rem(y + k, ny), y).start()
+    twin_line(y, core).start()
+    arrive(y, core)
+    for k in y_far[::-1]:
+        yy = lax.rem(y + k, ny)
+        line_copy(yy, yy).wait_recv()
+        twin_line(yy, core).start()
+        arrive(yy, core)
+    for k in [0] + y_far[::-1]:
+        yy = lax.rem(y + k, ny)
+        twin_line(yy, 1 - core).wait_recv()
+        arrive(yy, 1 - core)
 
     total_rows = parts * cuts
     chunk = 24
@@ -391,13 +412,9 @@
     chips = parts // nc
     chip = z * ny + y
     pair = pltpu.make_async_remote_copy(
-        tiles_ref.at[1 - core], pair_buf, ps, pr, device_id=(ga, at(z, y, 1 - core)), device_id_type=MESH
+        tiles_ref.at[1 - core], pair_buf, ps, pr, device_id=(ga, twin), device_id_type=MESH
     )
     pair.start()
-
-    def drain_row(k, c):
-        row_copy(far_first(k), me).wait_send()
-        return c
 
     for b in range(2):
         from_a = jnp.sum(a * meta[:, 2 + b : 3 + b], axis=0, keepdims=True)
@@ -408,22 +425,39 @@
     pair.wait_recv()
     sums[...] = tiles_ref[core] + pair_buf[...]
 
-    def part_copy(q):
-        return pltpu.make_async_remote_copy(
-            sums.at[q], got_ref.at[chip], ssem, rsem, device_id=(ga, q * nc + core), device_id_type=MESH
-        )
-
-    def send_part(k, c):
-        part_copy(lax.rem(chip + 1 + lax.rem(k + (chips * 5) // 16, chips - 1), chips)).start()
-        return c
-
-    lax.fori_loop(0, chips - 1, send_part, 0)
-    got_ref[chip] = sums[chip]
-    lax.fori_loop(0, others, drain_row, 0)
+    def y_part(yy):
+        return pltpu.make_async_remote_copy(
+            sums.at[pl.ds(yy * nz, nz)], y_got.at[y], ssem, rsem, device_id=(ga, at(z, yy, core)), device_id_type=MESH
+        )
+
+    for k in y_far:
+        y_part(lax.rem(y + k, ny)).start()
+    y_got[y] = sums[pl.ds(y * nz, nz)]
+    for k in z_far:
+        row_copy(lax.rem(z + k, nz), z).wait_send()
+    for k in y_far:
+        line_copy(lax.rem(y + k, ny), y).wait_send()
+    for yy in range(ny):
+        twin_line(yy, core).wait_send()
     for hop in hops:
         hop.wait_send()
     pair.wait_send()
-    settled((chips - 1) * per, rsem).wait_recv()
+    if ny > 1:
+        settled((ny - 1) * nz * per, rsem).wait_recv()
+    y_sum[...] = jnp.sum(y_got[...], axis=0)
+
+    def z_part(zz):
+        return pltpu.make_async_remote_copy(
+            y_sum.at[zz], got_ref.at[z], vs, vr, device_id=(ga, at(zz, y, core)), device_id_type=MESH
+        )
+
+    for k in z_far:
+        z_part(lax.rem(z + k, nz)).start()
+    got_ref[z] = y_sum[z]
+    if ny > 1:
+        settled((ny - 1) * nz * per, ssem).wait_send()
+    if nz > 1:
+        settled((nz - 1) * per, vr).wait_recv()
     zbuf[z] = jnp.sum(got_ref[...], axis=0)
 
     def z_copy(zz):
@@ -433,93 +467,33 @@
 
     for k in sorted(range(1, nz), key=lambda k: -min(k, nz - k)):
         z_copy(lax.rem(z + k, nz)).start()
-    settled((chips - 1) * per, ssem).wait_send()
+    if nz > 1:
+        settled((nz - 1) * per, vs).wait_send()
     if nz > 1:
         settled((nz - 1) * per, zr).wait_recv()
 
-    ring = groups
-    fx, fy = 1 - core, core
-
-    def along(first, second):
-        return (
-            lax.rem(ga + first * fx + second * fy + 2 * ring, ring),
-            lax.rem(y + first * fy + second * fx + 2 * ring, ring),
-        )
-
-    def piece(first, second, part):
-        aa, yy = along(first, second)
-        if part is None:
-            return gat.at[aa, yy, core]
-        return gat.at[aa, yy, core, pl.ds(part * (nz // 2), nz // 2)]
-
-    def push(src, first, second, to_first, to_second, sem, part=None):
-        aa, yy = along(to_first, to_second)
-        return pltpu.make_async_remote_copy(
-            src, piece(first, second, part), fs, fr.at[sem], device_id=(aa, at(z, yy, core)), device_id_type=MESH
-        )
-
-    def twin_copy(src, first, second):
-        return pltpu.make_async_remote_copy(
-            src, piece(first, second, None), cs, cr, device_id=(ga, at(z, y, 1 - core)), device_id_type=MESH
-        )
-
-    steps = [1] if ring == 2 else [-1, 1, 2]
-    sides = [1] if ring == 2 else [-1, 1]
-    row_of = [0] + steps
-
-    def sem_of(f, kind):
-        return f * 4 + kind
-
-    def own_block(f):
-        return zbuf if f == 0 else piece(row_of[f], 0, None)
-
-    def send_second(f):
-        for n, side in enumerate(sides):
-            push(own_block(f), row_of[f], 0, 0, side, sem_of(f, n)).start()
-
-    def await_first(n):
-        push(zbuf, steps[n], 0, 0, 1, 16 + n).wait_recv()
-        twin_copy(piece(steps[n], 0, None), steps[n], 0).start()
-        send_second(n + 1)
-
-    def await_second(f):
-        for n, side in enumerate(sides):
-            push(zbuf, row_of[f], -side, 0, side, sem_of(f, n)).wait_recv()
-            if ring == 4:
-                push(piece(row_of[f], -side, n), row_of[f], -side, 0, side, sem_of(f, 2 + n), n).start()
-            twin_copy(piece(row_of[f], -side, None), row_of[f], -side).start()
-
-    def await_halves(f):
-        if ring == 4:
-            for n in range(2):
-                push(piece(row_of[f], 2, n), row_of[f], 2, 0, 1, sem_of(f, 2 + n), n).wait_recv()
-            twin_copy(piece(row_of[f], 2, None), row_of[f], 2).start()
-
-    for n in range(len(steps) - 1, -1, -1):
-        back = steps[n] if ring == 2 else (steps[n] if steps[n] == 2 else -steps[n])
-        push(zbuf, 0, 0, back, 0, 16 + n).start()
-    send_second(0)
-    twin_copy(zbuf, 0, 0).start()
+    def plane_copy(src, aa, yy, slot_a, slot_y):
+        return pltpu.make_async_remote_copy(
+            src, gat.at[slot_a, slot_y, core], fs, fr.at[slot_a, slot_y],
+            device_id=(aa, at(z, yy, core)), device_id_type=MESH,
+        )
+
+    def twin_copy(src, slot_a, slot_y):
+        return pltpu.make_async_remote_copy(
+            src, gat.at[slot_a, slot_y, core], cs, cr,
+            device_id=(ga, at(z, y, 1 - core)), device_id_type=MESH,
+        )
+
+    for aa, yy, _ in around[::-1]:
+        plane_copy(zbuf, aa, yy, ga, y).start()
+    twin_copy(zbuf, ga, y).start()
     gat[ga, y, core] = zbuf[...]
-    if ring == 2:
-        await_first(0)
-        await_second(0)
-        await_second(1)
-    else:
-        await_first(0)
-        await_first(1)
-        await_second(0)
-        await_first(2)
-        await_second(1)
-        await_second(2)
-        await_halves(0)
-        await_second(3)
-        for f in (1, 2, 3):
-            await_halves(f)
-    sent = len(steps) * nz * per + len(row_of) * len(sides) * nz * per + (8 * (nz // 2) * per if ring == 4 else 0)
+    for aa, yy, _ in around:
+        plane_copy(zbuf, aa, yy, aa, yy).wait_recv()
+        twin_copy(gat.at[aa, yy, core], aa, yy).start()
     if nz > 1:
         settled((nz - 1) * per, zs).wait_send()
-    settled(sent, fs).wait_send()
+    settled((planes - 1) * nz * per, fs).wait_send()
     settled(planes * nz * per, cr).wait_recv()
     settled(planes * nz * per, cs).wait_send()
 
@@ -550,7 +524,7 @@
                 k = rg * 3 + lt
                 j, s = k // per, k % per
                 r_ref[g * ROWS + 8 * rg : g * ROWS + 8 * rg + 8, lt * LANES : (lt + 1) * LANES] = gat[
-                    g, (j // nc) % ny, j % nc, j // (ny * nc), s
+                    g, j // nc // nz, j % nc, (j // nc) % nz, s
                 ]
         ids = exc_ref[1, 2 * g : 2 * g + 2, :].astype(F32)
         p_row = packed_row(wide_ref.at[g], ids[0:1], ids[1:2], slots, float(pairs), float(pairs))
@@ -619,7 +593,7 @@
             pltpu.VMEM((cuts, slots_deep, LANES), F32),
             pltpu.VMEM((width, deep), I32),
             pltpu.VMEM((2 * cuts, LANES), F32),
-            pltpu.VMEM((parts, 2 * cuts, LANES), F32),
+            pltpu.VMEM((ny, nc, nz, 2 * cuts, LANES), F32),
             pltpu.VMEM((2, parts * cuts, 8, LANES), F32),
             pltpu.VMEM((2, parts * cuts, LANES), F32),
             pltpu.VMEM((2, cuts, slots_deep, LANES), F32),
@@ -629,14 +603,16 @@
             pltpu.VMEM((nc, parts // nc, per, 8, LANES), F32),
             pltpu.VMEM((parts // nc, per, 8, LANES), F32),
             pltpu.VMEM((parts // nc, per, 8, LANES), F32),
-            pltpu.VMEM((parts // nc, per, 8, LANES), F32),
+            pltpu.VMEM((ny, nz, per, 8, LANES), F32),
+            pltpu.VMEM((nz, per, 8, LANES), F32),
+            pltpu.VMEM((nz, per, 8, LANES), F32),
             pltpu.VMEM((nz, per, 8, LANES), F32),
             pltpu.VMEM((groups * ny * nz * per, 8, LANES), F32),
             dma((2,)),
-            dma((parts,)), dma((parts,)),
+            dma((nz,)), dma((nz,)), dma((ny,)), dma((ny,)), dma((ny,)), dma((ny,)), dma, dma,
             dma((4,)), dma((4,)),
             dma, dma, dma, dma, dma, dma, dma,
-            dma((20,)),
+            dma((groups, ny)),
             dma, dma,
         ],
         compiler_params=pltpu.CompilerParams(collective_id=0, has_side_effects=True),

time: 65.4 us -> 60.9 us (0.931)
  Pallas kernels: 64.6 us -> 60.1 us
    pallas_call x1, Pallas kernels: 60.1 us -> 55.5 us  [body(): pl.pallas_call(functools.partial(main_kernel, groups, shape, slots, pairs...]
where the time goes in v6:
time: 60.9 us; the launch traced here: 60.7 us
  Pallas kernels  60.1 us (99%)
  between operations  0.64 us (1%)
    pallas_call x1, Pallas kernels, body(): pl.pallas_call(functools.partial(main_kernel, groups, shape, slots, pairs...  55.5 us
    pallas_call x1, Pallas kernels, body(): pl.pallas_call(functools.partial(place_kernel, groups, shape, slots, pair...  4.55 us

profile of v6, /device:TPU:1, one launch (start us, length us, event | category | flops | bytes accessed | tf_op | source)
XLA Modules:
  0.0 60.7 jit_solution(5392962636938939310)
XLA Ops:
  0.6 55.5 %main.1 = (f32[2,384]{1,0:T(2,128)}, f32[4,4,2,8,1,8,128]{6,5,4,3,2,1,0:T(8,128)}) custom-call(s32[8]{0:T(128)} %batch_ref.1, s32[3,8,81]{2,1,0:T(8,128)} %exc_ref.3, s32[3,81,384]{2,1,0:T(8,128)} %bitcast.1, f32[324]{0:T(512)} %h_ref.1, f32[256,384]{1,0:T(8,128)} %civ_hbm.1), custom_call_target="tpu_custom_call" | custom-call | tf_op jit(solution)/shard_map/main/pallas_call | solution.py:579
  56.2 4.6 %place.1 = (f32[2,384]{1,0:T(2,128)}, f32[2,324]{1,0:T(2,128)}, f32[324,324]{1,0:T(8,128)}, f32[324,324]{1,0:T(8,128)}) custom-call(s32[3,8,81]{2,1,0:T(8,128)} %exc_ref.3, f32[4,4,2,8,1,8,128]{6,5,4,3,2,1,0:T(8,128)} %get-tuple-element.6.gat, f32[2,384]{1,0:T(2,128)} %get-tuple-element.7.sigma_in), custom_call_target="tpu_custom_call" | custom-call | tf_op jit(solution)/shard_map/place/pallas_call | solution.py:621

commit v7 on v6

--- a/solution.py
+++ b/solution.py
@@ -411,28 +411,31 @@
 
     chips = parts // nc
     chip = z * ny + y
-    pair = pltpu.make_async_remote_copy(
-        tiles_ref.at[1 - core], pair_buf, ps, pr, device_id=(ga, twin), device_id_type=MESH
-    )
-    pair.start()
-
-    for b in range(2):
-        from_a = jnp.sum(a * meta[:, 2 + b : 3 + b], axis=0, keepdims=True)
-        for lt in range(cuts):
-            cut = slice(lt * LANES, (lt + 1) * LANES)
-            from_b = jnp.sum(vals_ref[b, lt] * hx_ref[lt], axis=0, keepdims=True)
-            sigma_ref[b : b + 1, cut] = from_a[:, cut] + from_b
-    pair.wait_recv()
-    sums[...] = tiles_ref[core] + pair_buf[...]
+    def pair_copy(yy):
+        rows = pl.ds(yy * nz, nz)
+        return pltpu.make_async_remote_copy(
+            tiles_ref.at[1 - core, rows], pair_buf.at[rows], ps.at[yy], pr.at[yy],
+            device_id=(ga, twin), device_id_type=MESH,
+        )
+
+    turns = [lax.rem(y + k, ny) for k in y_far] + [y]
+    for yy in turns:
+        pair_copy(yy).start()
 
     def y_part(yy):
         return pltpu.make_async_remote_copy(
             sums.at[pl.ds(yy * nz, nz)], y_got.at[y], ssem, rsem, device_id=(ga, at(z, yy, core)), device_id_type=MESH
         )
 
-    for k in y_far:
-        y_part(lax.rem(y + k, ny)).start()
-    y_got[y] = sums[pl.ds(y * nz, nz)]
+    for k, yy in enumerate(turns):
+        rows = pl.ds(yy * nz, nz)
+        pair_copy(yy).wait_recv()
+        part = tiles_ref[core, rows] + pair_buf[rows]
+        if k < len(y_far):
+            sums[rows] = part
+            y_part(yy).start()
+        else:
+            y_got[y] = part
     for k in z_far:
         row_copy(lax.rem(z + k, nz), z).wait_send()
     for k in y_far:
@@ -441,7 +444,14 @@
         twin_line(yy, core).wait_send()
     for hop in hops:
         hop.wait_send()
-    pair.wait_send()
+    for yy in range(ny):
+        pair_copy(yy).wait_send()
+    for b in range(2):
+        from_a = jnp.sum(a * meta[:, 2 + b : 3 + b], axis=0, keepdims=True)
+        for lt in range(cuts):
+            cut = slice(lt * LANES, (lt + 1) * LANES)
+            from_b = jnp.sum(vals_ref[b, lt] * hx_ref[lt], axis=0, keepdims=True)
+            sigma_ref[b : b + 1, cut] = from_a[:, cut] + from_b
     if ny > 1:
         settled((ny - 1) * nz * per, rsem).wait_recv()
     y_sum[...] = jnp.sum(y_got[...], axis=0)
@@ -611,7 +621,7 @@
             dma((2,)),
             dma((nz,)), dma((nz,)), dma((ny,)), dma((ny,)), dma((ny,)), dma((ny,)), dma, dma,
             dma((4,)), dma((4,)),
-            dma, dma, dma, dma, dma, dma, dma,
+            dma((ny,)), dma((ny,)), dma, dma, dma, dma, dma,
             dma((groups, ny)),
             dma, dma,
         ],

time: 60.9 us -> 60.8 us (level)
  no operation moved by 1% of the time
where the time goes in v7:
time: 60.8 us; the launch traced here: 60.6 us
  Pallas kernels  60 us (99%)
  between operations  0.64 us (1%)
    pallas_call x1, Pallas kernels, body(): pl.pallas_call(functools.partial(main_kernel, groups, shape, slots, pairs...  55.4 us
    pallas_call x1, Pallas kernels, body(): pl.pallas_call(functools.partial(place_kernel, groups, shape, slots, pair...  4.55 us

profile of v7, /device:TPU:1, one launch (start us, length us, event | category | flops | bytes accessed | tf_op | source)
XLA Modules:
  0.0 60.6 jit_solution(16552842323892097096)
XLA Ops:
  0.6 55.4 %main.1 = (f32[2,384]{1,0:T(2,128)}, f32[4,4,2,8,1,8,128]{6,5,4,3,2,1,0:T(8,128)}) custom-call(s32[8]{0:T(128)} %batch_ref.1, s32[3,8,81]{2,1,0:T(8,128)} %exc_ref.3, s32[3,81,384]{2,1,0:T(8,128)} %bitcast.1, f32[324]{0:T(512)} %h_ref.1, f32[256,384]{1,0:T(8,128)} %civ_hbm.1), custom_call_target="tpu_custom_call" | custom-call | tf_op jit(solution)/shard_map/main/pallas_call | solution.py:589
  56.0 4.6 %place.1 = (f32[2,384]{1,0:T(2,128)}, f32[2,324]{1,0:T(2,128)}, f32[324,324]{1,0:T(8,128)}, f32[324,324]{1,0:T(8,128)}) custom-call(s32[3,8,81]{2,1,0:T(8,128)} %exc_ref.3, f32[4,4,2,8,1,8,128]{6,5,4,3,2,1,0:T(8,128)} %get-tuple-element.6.gat, f32[2,384]{1,0:T(2,128)} %get-tuple-element.7.sigma_in), custom_call_target="tpu_custom_call" | custom-call | tf_op jit(solution)/shard_map/place/pallas_call | solution.py:631
